TPU v7x, 512 devices: a whole 4x4x16 slice. The times are simulated.
512 devices in a mesh: dp: 64 (over z, x), seq: 8 (over y, core).
Axes of the slice: x: 4, y: 4, z: 16, core: 2. Of those that a mesh axis runs over, the one named last changes fastest.
Arguments:
- events: bfloat16 [64, 2048, 1024], P('dp', 'seq')
- w_project: bfloat16 [1024, 4096], P(None, 'seq'), may hold values from -0.1875 to 0.1875
- w_output: bfloat16 [1024, 1024], P('seq'), may hold values from -0.1875 to 0.1875
- rel_bias: float32 [8, 11], P('seq'), may hold values from -4 to 4
- in_gain: float32 [1024], replicated, may hold values from 0.5 to 1.5
- out_gain: float32 [1024], P('seq'), may hold values from 0.5 to 1.5
- user_ids: int32 [64, 2048], P('dp'), may hold values from 0 to 3, never falling along the last dimension, each value on 1 to 1024 neighbouring positions
- owner_dev: int32 [64, 2048], P('dp', 'seq'), may hold values from 0 to 63, as said below
- owner_row: int32 [64, 2048], P('dp', 'seq'), may hold values from 0 to 255, as said below
Outputs:
- layer_update: bfloat16 [64, 2048, 1024], P('dp', 'seq')
Inputs may be any that keep to these rules, and one draw needn't show every extreme that they name: `owner_dev`: within each index of seq, a device sends to one index of dp either none of its rows or exactly 4 of them, and every device receives exactly 256 rows. `owner_row`: the owner rows that reach one device from all indices of dp are distinct and cover 0 to 255. `user_ids`: along the 2048 rows of each dp index the user number never falls; each user has 1 to 1024 rows and one has exactly 1024.
All inputs are finite; a program needn't handle non-finite values.
Results may differ from a plain program's by a relative error of at most 0.014.
Values may be sent and summed in bfloat16 or wider, within the bound.
A program may use at most 64 MiB of HBM per device.

v0:
```python
import jax
import jax.numpy as jnp
from jax import lax
from jax.sharding import PartitionSpec as P

EPSILON = 1e-05


def norm_rows(values, gain):
    average = jnp.mean(values, axis=-1, keepdims=True)
    centred = values - average
    spread = jnp.mean(centred * centred, axis=-1, keepdims=True)
    return centred * lax.rsqrt(spread + EPSILON) * gain


def bucket_bias(table, distance, longest):
    levels = table.shape[0]
    total = jnp.zeros(distance.shape, jnp.float32) + table[0]
    for level in range(levels - 1):
        threshold = longest // 2 ** (levels - 1 - level)
        total = total + jnp.where(
            distance >= threshold, table[level + 1] - table[level], jnp.zeros((), jnp.float32)
        )
    return total


def head_block(queries, key_rows, values, query_first, table, segment, longest):
    tile_rows = queries.shape[0]
    key_count = key_rows.shape[0]
    distance = (query_first + jnp.arange(tile_rows, dtype=jnp.int32))[:, None] - jnp.arange(
        key_count, dtype=jnp.int32
    )[None, :]
    query_users = segment[query_first : query_first + tile_rows]
    alive = (distance >= 0) & (query_users[:, None] == segment[None, :])
    scores = jnp.dot(queries, key_rows.T, preferred_element_type=jnp.float32) * queries.shape[
        1
    ] ** (-0.5) + bucket_bias(table, distance, longest)
    weights = jnp.where(alive, jax.nn.silu(scores), jnp.zeros((), jnp.float32)).astype(jnp.bfloat16)
    return jnp.dot(weights, values, preferred_element_type=jnp.float32)


def local(events, w_project, w_output, rel_bias, in_gain, out_gain, user_ids, owner_dev, owner_row):
    peer_count = lax.axis_size("dp")
    row_count = events.shape[1]
    feat_width = events.shape[2]
    capacity = max(2, row_count // peer_count)
    owners = owner_dev[0]
    places = owner_row[0]
    one_hot = (owners[:, None] == jnp.arange(peer_count, dtype=jnp.int32)[None, :]).astype(
        jnp.int32
    )
    earlier = jnp.cumsum(one_hot, axis=0) - one_hot
    send_slot = owners * capacity + jnp.sum(earlier * one_hot, axis=1)
    send_rows = (
        jnp.zeros((peer_count * capacity, feat_width), jnp.bfloat16).at[send_slot].set(events[0])
    )
    send_place = jnp.full((peer_count * capacity,), row_count, jnp.int32).at[send_slot].set(places)
    got_rows, got_place = (
        lax.all_to_all(
            send_rows.reshape(peer_count, capacity, feat_width),
            "dp",
            split_axis=0,
            concat_axis=0,
            tiled=True,
        ),
        lax.all_to_all(
            send_place.reshape(peer_count, capacity), "dp", split_axis=0, concat_axis=0, tiled=True
        ),
    )
    flat_place = got_place.reshape(-1)
    owned = (
        jnp.zeros((row_count, feat_width), jnp.bfloat16)
        .at[flat_place]
        .set(got_rows.reshape(-1, feat_width), mode="drop")
    )
    normed = norm_rows(owned.astype(jnp.float32), in_gain).astype(jnp.bfloat16)
    projected = jax.nn.silu(
        jnp.dot(
            lax.all_gather(normed, "seq", axis=0, tiled=True),
            w_project,
            preferred_element_type=jnp.float32,
        )
    ).astype(jnp.bfloat16)
    all_rows = projected.shape[0]
    longest = all_rows // 2
    local_heads = rel_bias.shape[0]
    head_width = w_output.shape[0] // local_heads
    projected = projected.reshape(all_rows, local_heads, 4, head_width)
    segment = user_ids[0]
    tile_rows = min(512, all_rows)
    block_count = all_rows // tile_rows
    queries = projected[:, 0, 0]
    key_rows = projected[:, 0, 1]
    values = projected[:, 0, 2]
    gate_rows = projected[:, 0, 3]
    table = rel_bias[0]
    blocks_out = []
    for query_blk in range(block_count):
        query_first = query_blk * tile_rows
        query_rows = queries[query_first : query_first + tile_rows]
        mixed = head_block(query_rows, key_rows, values, query_first, table, segment, longest)
        gate_block = gate_rows[query_first : query_first + tile_rows].astype(jnp.float32)
        blocks_out.append((norm_rows(mixed, out_gain) * gate_block).astype(jnp.bfloat16))
    head_outputs = jnp.concatenate(blocks_out, axis=0)
    term = jnp.dot(head_outputs, w_output, preferred_element_type=jnp.float32)
    merged = lax.psum_scatter(
        lax.optimization_barrier(term.astype(jnp.bfloat16))
        .astype(jnp.float32)
        .astype(jnp.bfloat16),
        "seq",
        scatter_dimension=0,
        tiled=True,
    )
    returned_rows = merged[jnp.clip(flat_place, 0, row_count - 1)].reshape(
        peer_count, capacity, feat_width
    )
    home_rows = lax.all_to_all(returned_rows, "dp", split_axis=0, concat_axis=0, tiled=True)
    return home_rows.reshape(-1, feat_width)[send_slot][None]


def solution(mesh):
    return jax.shard_map(
        local,
        mesh=mesh,
        in_specs=(
            P("dp", "seq", None),
            P(None, "seq"),
            P("seq", None),
            P("seq", None),
            P(),
            P("seq"),
            P("dp", None),
            P("dp", "seq"),
            P("dp", "seq"),
        ),
        out_specs=P("dp", "seq", None),
        check_vma=False,
    )
```

profile of v0, /device:TPU:25, one launch (start us, length us, event | category | flops | bytes accessed | tf_op | source)
XLA Modules:
  0.0 258.5 jit_solution(3112857160965579812)
XLA Ops:
  6.5 0.0 copy-start
  6.5 0.0 copy-start.5
  6.5 0.0 copy-start.3
  6.5 0.0 copy-start.4
  6.5 0.8 fusion.76
  7.3 0.6 reduce-window.6
  7.9 0.2 slice_reduce_fusion
  8.2 0.8 fusion.75
  8.9 0.7 compare_select_fusion.2
  9.6 1.6 scatter_custom_fusion
  11.2 0.7 all_to_all.12
  11.9 18.3 %all-to-all-start = ((s32[64,1,4]{2,1,0:T(1,128)}), s32[64,1,4]{2,1,0:T(1,128)S(1)}, u32[]{:S(2)}, u32[]{:S(2)}) async-start(s32[64,1,4]{2,1,0:T(1,128)} %bitcast.9), calls=%async_computation | async-start | bytes 65536 | tf_op jit(solution)/shard_map/all_to_all | solution.py:66
  30.2 2.3 scatter_custom_fusion.1
  32.5 1.0 reshape.242
  33.5 10.3 %all-to-all-done = s32[64,1,4]{2,1,0:T(1,128)S(1)} async-done(((s32[64,1,4]{2,1,0:T(1,128)}), s32[64,1,4]{2,1,0:T(1,128)S(1)}, u32[]{:S(2)}, u32[]{:S(2)}) %all-to-all-start) | async-done | bytes 1056 | tf_op jit(solution)/shard_map/all_to_all | solution.py:66
  43.8 4.6 %all-to-all-start.1 = ((bf16[64,4,1024]{2,1,0:T(4,128)(2,1)}), bf16[64,4,1024]{2,1,0:T(4,128)(2,1)S(1)}, u32[]{:S(2)}, u32[]{:S(2)}) async-start(bf16[64,4,1024]{2,1,0:T(4,128)(2,1)} %reshape.242), calls=%async_computation.1 | async-start | bytes 1048576 | tf_op jit(solution)/shard_map/all_to_all | solution.py:59
  48.4 0.0 all-gather.2.cloned.1.call-start
  48.5 0.6 broadcast.446
  49.1 0.8 reduce.5
  49.9 0.1 reshape.241
  50.0 27.5 %all-to-all-done.1 = bf16[64,4,1024]{2,1,0:T(4,128)(2,1)S(1)} async-done(((bf16[64,4,1024]{2,1,0:T(4,128)(2,1)}), bf16[64,4,1024]{2,1,0:T(4,128)(2,1)S(1)}, u32[]{:S(2)}, u32[]{:S(2)}) %all-to-all-start.1) | async-done | bytes 524320 | tf_op jit(solution)/shard_map/all_to_all | solution.py:59
  77.5 0.1 reshape.287
  77.6 1.8 scatter_custom_fusion.2
  79.4 0.1 convert_reduce_fusion
  79.6 0.3 fusion.54
  79.9 0.0 copy-done.5
  79.9 1.1 fusion.56
  81.0 0.0 all-gather.2.cloned.1.call-update
  81.0 0.2 reduce-scatter.2.cloned.1.call-start
  81.2 0.0 copy-done.3
  81.2 0.7 fusion.137
  94.2 0.0 copy-done.4
  94.2 20.8 %all-gather.2.cloned.1.call-done = bf16[2048,1024]{1,0:T(8,128)(2,1)} async-done(((bf16[256,1024]{1,0:T(8,128)(2,1)}), bf16[2048,1024]{1,0:T(8,128)(2,1)}) %all-gather.2.cloned.1.call-update) | async-done | bytes 4194320 | tf_op jit(solution)/shard_map/all_gather | solution.py:79
  114.9 0.0 copy-done
  114.9 5.2 %multiply_convert_fusion = bf16[2048,512]{0,1:T(8,128)(2,1)S(1)} fusion(bf16[2048,1024]{1,0:T(8,128)(2,1)} %all-gather.2.cloned.1.call-done, bf16[1024,512]{1,0:T(8,128)(2,1)S(1)} %copy-done), kind=kOutput, calls=%fused_computation.45 | convolution fusion | flops 2152726528 | bytes 7340032 | tf_op jit(solution)/shard_map/dot_general | solution.py:78
  120.2 0.0 copy-start.2
  120.2 7.0 %fusion.139 = (f32[512]{0:T(512)S(1)}, f32[512,128]{0,1:T(8,128)S(1)}) fusion(bf16[2048,1,4,128]{0,3,2,1:T(8,128)(2,1)S(1)} %bitcast.131, s32[512]{0:T(512)S(1)} %iota_add_fusion.1, f32[]{:T(128)S(6)} %sub.410, f32[]{:T(128)S(6)} %sub.409, f32[]{:T(128)S(6)} %sub.408, f32[]{:T(128)S(6)} %sub.407, f32[]{:T(128)S(6)} %sub.406, f32[]{:T(128)S(6)} %sub.405, ...), kind=kOutput, calls=%fused_computation.198 | convolution fusion | flops 580976128 | bytes 1456172 | tf_op jit(solution)/shard_map/dot_general | solution.py:39
  127.2 0.0 copy-done.2
  127.2 8.4 %fusion.141 = (f32[512]{0:T(512)S(1)}, f32[512,128]{0,1:T(8,128)S(1)}) fusion(bf16[2048,1,4,128]{0,3,2,1:T(8,128)(2,1)} %bitcast.132, s32[512]{0:T(512)S(1)} %iota_add_fusion, f32[]{:T(128)S(6)} %sub.410, f32[]{:T(128)S(6)} %sub.409, f32[]{:T(128)S(6)} %sub.408, f32[]{:T(128)S(6)} %sub.407, f32[]{:T(128)S(6)} %sub.406, f32[]{:T(128)S(6)} %sub.405, ...), kind=kOutput, calls=%fused_computation.200 | convolution fusion | flops 580976128 | bytes 1456680 | tf_op jit(solution)/shard_map/dot_general | solution.py:39
  135.6 3.2 %fusion.138 = (f32[512]{0:T(512)S(1)}, f32[512,128]{0,1:T(8,128)S(1)}) fusion(bf16[2048,1,4,128]{0,3,2,1:T(8,128)(2,1)} %bitcast.133, f32[]{:T(128)S(6)} %sub.410, f32[]{:T(128)S(6)} %sub.409, f32[]{:T(128)S(6)} %sub.408, f32[]{:T(128)S(6)} %sub.407, f32[]{:T(128)S(6)} %sub.406, f32[]{:T(128)S(6)} %sub.405, f32[]{:T(128)S(6)} %sub.404, f32[]{:T(128)S(6)} %sub.403, ...), kind=kOutput, calls=%fused_computation.197 | convolution fusion | flops 580976128 | bytes 1454632 | tf_op jit(solution)/shard_map/dot_general | solution.py:39
  138.8 0.0 copy-start.6
  138.8 0.0 copy-start.1
  138.8 8.2 %fusion.140 = (f32[512]{0:T(512)S(1)}, f32[512,128]{0,1:T(8,128)S(1)}) fusion(bf16[2048,1,4,128]{0,3,2,1:T(8,128)(2,1)} %bitcast.134, s32[512]{0:T(512)S(1)} %iota_add_fusion.2, f32[]{:T(128)S(6)} %sub.410, f32[]{:T(128)S(6)} %sub.409, f32[]{:T(128)S(6)} %sub.408, f32[]{:T(128)S(6)} %sub.407, f32[]{:T(128)S(6)} %sub.406, f32[]{:T(128)S(6)} %sub.405, ...), kind=kOutput, calls=%fused_computation.199 | convolution fusion | flops 580976128 | bytes 1456680 | tf_op jit(solution)/shard_map/dot_general | solution.py:39
  147.1 0.1 multiply_reduce_fusion.1
  147.2 0.1 multiply_reduce_fusion
  147.2 0.1 multiply_reduce_fusion.3
  147.3 0.0 copy-done.6
  147.3 1.4 fusion.69
  148.7 0.0 copy-done.1
  148.8 3.5 %convolution_convert_fusion = bf16[2048,1024]{1,0:T(8,128)(2,1)} fusion(bf16[128,1024]{1,0:T(8,128)(2,1)S(1)} %copy-done.1, bf16[512,128]{0,1:T(8,128)(2,1)S(1)} %get-tuple-element.8, bf16[512,128]{0,1:T(8,128)(2,1)S(1)} %get-tuple-element.6, bf16[512,128]{0,1:T(8,128)(2,1)S(1)} %get-tuple-element.7, bf16[512,128]{0,1:T(8,128)(2,1)S(1)} %get-tuple-element.5), kind=kOutput, calls=%fused_computation.62 | convolution fusion | flops 541065216 | bytes 4980736 | tf_op jit(solution)/shard_map/dot_general | solution.py:105
  152.2 0.0 reduce-scatter.2.cloned.1.call-update
  152.2 46.5 %reduce-scatter.2.cloned.1.call-done = bf16[256,1024]{1,0:T(8,128)(2,1)} async-done(((bf16[2048,1024]{1,0:T(8,128)(2,1)}), bf16[256,1024]{1,0:T(8,128)(2,1)}) %reduce-scatter.2.cloned.1.call-update) | async-done | bytes 524304 | tf_op jit(solution)/shard_map/reduce_scatter | solution.py:106
  198.7 2.7 %gather_fusion = bf16[256,1024]{1,0:T(8,128)(2,1)S(1)} fusion(bf16[256,1024]{1,0:T(8,128)(2,1)} %reduce-scatter.2.cloned.1.call-done, s32[1024]{0:T(1024)S(1)} %pad_clamp_fusion.1), kind=kCustom, calls=%fused_computation | custom fusion | bytes 1049600 | tf_op jit(solution)/shard_map/gather | solution.py:114
  201.4 1.0 reshape.245
  202.4 14.6 %all-to-all-start.2 = ((bf16[64,4,1024]{2,1,0:T(4,128)(2,1)}), bf16[64,4,1024]{2,1,0:T(4,128)(2,1)S(1)}, u32[]{:S(2)}, u32[]{:S(2)}) async-start(bf16[64,4,1024]{2,1,0:T(4,128)(2,1)} %reshape.245), calls=%async_computation.3 | async-start | bytes 1048576 | tf_op jit(solution)/shard_map/all_to_all | solution.py:117
  217.0 32.5 %all-to-all-done.2 = bf16[64,4,1024]{2,1,0:T(4,128)(2,1)S(1)} async-done(((bf16[64,4,1024]{2,1,0:T(4,128)(2,1)}), bf16[64,4,1024]{2,1,0:T(4,128)(2,1)S(1)}, u32[]{:S(2)}, u32[]{:S(2)}) %all-to-all-start.2) | async-done | bytes 524320 | tf_op jit(solution)/shard_map/all_to_all | solution.py:117
  249.5 0.1 reshape.246
  249.7 2.0 gather_fusion.1
  (18 shorter events, 0.2 us)
Async XLA Ops:
  6.5 108.4 %copy-start = (bf16[1024,512]{1,0:T(8,128)(2,1)S(1)}, bf16[1024,512]{1,0:T(8,128)(2,1)}, u32[]{:S(2)}) copy-start(bf16[1024,512]{1,0:T(8,128)(2,1)} %param.10) | copy-start | bytes 3145732
  6.5 73.3 %copy-start.5 = (f32[1024]{0:T(1024)S(1)}, f32[1024]{0:T(1024)}, u32[]{:S(2)}) copy-start(f32[1024]{0:T(1024)} %param.13) | copy-start | bytes 12292
  6.5 74.7 %copy-start.3 = (f32[1,11]{1,0:T(1,128)S(1)}, f32[1,11]{1,0:T(1,128)}, u32[]{:S(2)}) copy-start(f32[1,11]{1,0:T(1,128)} %param.12) | copy-start | bytes 136
  6.5 87.6 %copy-start.4 = (s32[1,2048]{1,0:T(1,128)S(1)}, s32[1,2048]{1,0:T(1,128)}, u32[]{:S(2)}) copy-start(s32[1,2048]{1,0:T(1,128)} %param.15) | copy-start | bytes 24580
  11.9 31.9 %all-to-all-start = ((s32[64,1,4]{2,1,0:T(1,128)}), s32[64,1,4]{2,1,0:T(1,128)S(1)}, u32[]{:S(2)}, u32[]{:S(2)}) async-start(s32[64,1,4]{2,1,0:T(1,128)} %bitcast.9), calls=%async_computation | async-start | bytes 65536 | tf_op jit(solution)/shard_map/all_to_all | solution.py:66
  43.8 33.7 %all-to-all-start.1 = ((bf16[64,4,1024]{2,1,0:T(4,128)(2,1)}), bf16[64,4,1024]{2,1,0:T(4,128)(2,1)S(1)}, u32[]{:S(2)}, u32[]{:S(2)}) async-start(bf16[64,4,1024]{2,1,0:T(4,128)(2,1)} %reshape.242), calls=%async_computation.1 | async-start | bytes 1048576 | tf_op jit(solution)/shard_map/all_to_all | solution.py:59
  48.4 66.5 %all-gather.2.cloned.1.call-start = ((), (), s32[]{:S(2)}) async-start(), calls=%async_computation.4 | async-start | bytes 4718592 | tf_op jit(solution)/shard_map/all_gather | solution.py:79
  81.0 117.7 %reduce-scatter.2.cloned.1.call-start = ((), (), s32[]{:S(2)}) async-start(), calls=%async_computation.5 | async-start | bytes 4718592 | tf_op jit(solution)/shard_map/reduce_scatter | solution.py:106
  120.2 7.0 %copy-start.2 = (bf16[2048,512]{0,1:T(8,128)(2,1)}, bf16[2048,512]{0,1:T(8,128)(2,1)S(1)}, u32[]{:S(2)}) copy-start(bf16[2048,512]{0,1:T(8,128)(2,1)S(1)} %multiply_convert_fusion) | copy-start | bytes 6291460
  138.8 8.5 %copy-start.6 = (f32[128]{0:T(128)S(1)}, f32[128]{0:T(128)}, u32[]{:S(2)}) copy-start(f32[128]{0:T(128)} %param.14) | copy-start | bytes 1540
  138.8 9.9 %copy-start.1 = (bf16[128,1024]{1,0:T(8,128)(2,1)S(1)}, bf16[128,1024]{1,0:T(8,128)(2,1)}, u32[]{:S(2)}) copy-start(bf16[128,1024]{1,0:T(8,128)(2,1)} %param.11) | copy-start | bytes 786436
  202.4 47.1 %all-to-all-start.2 = ((bf16[64,4,1024]{2,1,0:T(4,128)(2,1)}), bf16[64,4,1024]{2,1,0:T(4,128)(2,1)S(1)}, u32[]{:S(2)}, u32[]{:S(2)}) async-start(bf16[64,4,1024]{2,1,0:T(4,128)(2,1)} %reshape.245), calls=%async_computation.3 | async-start | bytes 1048576 | tf_op jit(solution)/shard_map/all_to_all | solution.py:117
Sparse Core Ops, SparseCore 0:
  81.1 33.7 all-gather.1
  152.3 46.3 reduce-scatter.1
where the time goes:
time: 259 us; the launch traced here: 258 us
  waiting for transfers between devices  138 us (53%)
  starting transfers between devices  37.7 us (15%)
  matrix products  35.5 us (14%)
  between operations  25.9 us (10%)
  local copies, waits for them, and re-layouts  14.8 us (6%)
  other arithmetic  6.86 us (3%)
    reduce_scatter x1, waiting for transfers between devices, local(): lax.psum_scatter(lax.optimization_barrier(term.astype(jnp.bfloat16)).asty...  46.5 us
    all_to_all x1, waiting for transfers between devices, local(): lax.all_to_all(returned_rows, 'dp', split_axis=0, concat_axis=0, tiled=True)  32.5 us
    all_to_all x1, waiting for transfers between devices, local(): lax.all_to_all(send_rows.reshape(peer_count, capacity, feat_width), 'dp',...  27.5 us
    dot_general x4, matrix products, head_block(): return jnp.dot(weights, values, preferred_element_type=jnp.float32)  26.8 us
    all_gather x1, waiting for transfers between devices, local(): lax.all_gather(normed, 'seq', axis=0, tiled=True)  20.8 us
    all_to_all x1, starting transfers between devices, local(): lax.all_to_all(send_place.reshape(peer_count, capacity), 'dp', split_axis...  18.3 us
    all_to_all x1, starting transfers between devices, local(): lax.all_to_all(returned_rows, 'dp', split_axis=0, concat_axis=0, tiled=True)  14.6 us
    all_to_all x1, waiting for transfers between devices, local(): lax.all_to_all(send_place.reshape(peer_count, capacity), 'dp', split_axis...  10.3 us
  transfers between devices with their start and end apart: 5, of which 5 were waited for; matrix products, arithmetic and copies ran while one was open for 2% of the time, Pallas kernels for 0%

commit v1 on v0

v1 whole, which is shorter than its diff:
```python
import jax
import jax.numpy as jnp
from jax import lax
from jax.experimental import pallas as pl
from jax.experimental.pallas import tpu as pltpu
from jax.sharding import PartitionSpec as P

EPSILON = 1e-05
BLOCK = 256
FAR = -1e30


def norm_rows(values, gain):
    average = jnp.mean(values, axis=-1, keepdims=True)
    centred = values - average
    spread = jnp.mean(centred * centred, axis=-1, keepdims=True)
    return centred * lax.rsqrt(spread + EPSILON) * gain


def half_silu(half):
    return half + half * jnp.tanh(half)


def half_bias(table, offset, longest, levels):
    rows = lax.broadcasted_iota(jnp.int32, (BLOCK, BLOCK), 0)
    columns = lax.broadcasted_iota(jnp.int32, (BLOCK, BLOCK), 1)
    distance = rows - columns + offset * BLOCK
    total = jnp.full((BLOCK, BLOCK), table[0, 0], jnp.float32)
    for level in range(levels - 1):
        threshold = longest // 2 ** (levels - 1 - level)
        step = table[0, level + 1] - table[0, level]
        if threshold > offset * BLOCK + BLOCK - 1:
            continue
        if threshold <= offset * BLOCK - BLOCK + 1:
            total = total + step
        else:
            total = total + jnp.where(distance >= threshold, step, 0.0)
    total = 0.5 * total
    if offset == 0:
        total = jnp.where(distance >= 0, total, FAR)
    return total


def head_kernel(longest, table, x_ref, w_ref, gain_ref, row_ids, col_ids, out_ref, proj, bias, acc):
    step = pl.program_id(0)
    reach = bias.shape[0]
    width = acc.shape[1]

    @pl.when(step == 0)
    def _():
        for offset in range(reach):
            bias[offset] = half_bias(table, offset, longest, table.shape[1])

    here = pl.ds(pl.multiple_of(step * BLOCK, BLOCK), BLOCK)
    proj[here, :] = half_silu(
        0.5 * jnp.dot(x_ref[...], w_ref[...], preferred_element_type=jnp.float32)
    ).astype(jnp.bfloat16)
    ids = jnp.concatenate([col_ids[...]] * (BLOCK // col_ids.shape[1]), axis=1)
    scale = 0.5 * width ** (-0.5)

    def term(offset):
        first = pl.multiple_of((step - offset) * BLOCK, BLOCK)
        there = pl.ds(first, BLOCK)
        scores = lax.dot_general(
            proj[here, :width],
            proj[there, width : 2 * width],
            (((1,), (1,)), ((), ())),
            preferred_element_type=jnp.float32,
        )
        weights = half_silu(scores * scale + bias[offset])
        weights = jnp.where(ids == row_ids[:, there], weights, 0.0).astype(jnp.bfloat16)
        return jnp.dot(
            weights, proj[there, 2 * width : 3 * width], preferred_element_type=jnp.float32
        )

    acc[...] = term(0)
    for offset in range(1, reach):

        @pl.when(step >= offset)
        def _(offset=offset):
            acc[...] += term(offset)

    gate = proj[here, 3 * width :].astype(jnp.float32)
    out_ref[...] = (norm_rows(acc[...], gain_ref[...]) * gate).astype(jnp.bfloat16)


def heads(rows, w_project, table, gain, segment, longest):
    count, depth = rows.shape
    width = gain.shape[0]
    reach = longest // BLOCK + 1
    return pl.pallas_call(
        lambda *refs: head_kernel(longest, *refs),
        grid=(count // BLOCK,),
        out_shape=jax.ShapeDtypeStruct((count, width), jnp.bfloat16),
        in_specs=[
            pl.BlockSpec(memory_space=pltpu.SMEM),
            pl.BlockSpec((BLOCK, depth), lambda i: (i, 0)),
            pl.BlockSpec((depth, 4 * width), lambda i: (0, 0)),
            pl.BlockSpec((1, width), lambda i: (0, 0)),
            pl.BlockSpec((1, count), lambda i: (0, 0)),
            pl.BlockSpec((BLOCK, 128), lambda i: (i, 0)),
        ],
        out_specs=pl.BlockSpec((BLOCK, width), lambda i: (i, 0)),
        scratch_shapes=[
            pltpu.VMEM((count, 4 * width), jnp.bfloat16),
            pltpu.VMEM((reach, BLOCK, BLOCK), jnp.float32),
            pltpu.VMEM((BLOCK, width), jnp.float32),
        ],
        compiler_params=pltpu.CompilerParams(vmem_limit_bytes=32 << 20),
    )(
        table,
        rows,
        w_project,
        gain[None],
        segment,
        jnp.broadcast_to(segment.reshape(count, 1), (count, 128)),
    )


def pick(chosen, rows, dim):
    return lax.dot_general(
        chosen, rows, (((dim,), (0,)), ((), ())), preferred_element_type=jnp.float32
    ).astype(jnp.bfloat16)


def local(events, w_project, w_output, rel_bias, in_gain, out_gain, user_ids, owner_dev, owner_row):
    peers = lax.axis_size("dp")
    parts = lax.axis_size("seq")
    count, depth = events.shape[1:]
    each = count // peers
    owners = owner_dev[0]
    index = jnp.arange(count, dtype=jnp.int32)
    earlier = (owners[:, None] == owners[None, :]) & (index[None, :] < index[:, None])
    slot = owners * each + jnp.sum(earlier.astype(jnp.int32), axis=1)
    to_slot = (slot[None, :] == index[:, None]).astype(jnp.bfloat16)
    tagged = jnp.concatenate(
        [events[0], jnp.broadcast_to(owner_row[0][:, None], (count, 128)).astype(jnp.bfloat16)], axis=1
    )
    sent = pick(to_slot, tagged, 1)
    w_full = lax.all_gather(w_output, "seq", axis=0, tiled=True)
    got = lax.all_to_all(
        sent.reshape(peers, each, depth + 128), "dp", split_axis=0, concat_axis=0, tiled=True
    ).reshape(count, depth + 128)
    place = got[:, depth].astype(jnp.int32)
    to_place = (place[:, None] == index[None, :]).astype(jnp.bfloat16)
    normed = norm_rows(got[:, :depth].astype(jnp.float32), in_gain).astype(jnp.bfloat16)
    normed = pick(to_place, normed, 0)
    rows = lax.all_gather(normed, "seq", axis=0, tiled=True)
    gated = heads(rows, w_project, rel_bias, out_gain, user_ids, count * parts // 2)
    mine = lax.all_to_all(
        gated.reshape(parts, count, -1), "seq", split_axis=0, concat_axis=0, tiled=True
    )
    merged = jnp.einsum(
        "hrd,hdo->ro",
        mine,
        w_full.reshape(parts, -1, depth),
        preferred_element_type=jnp.float32,
    ).astype(jnp.bfloat16)
    returned = pick(to_place, merged, 1)
    home = lax.all_to_all(
        returned.reshape(peers, each, depth), "dp", split_axis=0, concat_axis=0, tiled=True
    ).reshape(count, depth)
    return pick(to_slot, home, 0)[None]


def solution(mesh):
    return jax.shard_map(
        local,
        mesh=mesh,
        in_specs=(
            P("dp", "seq", None),
            P(None, "seq"),
            P("seq", None),
            P("seq", None),
            P(),
            P("seq"),
            P("dp", None),
            P("dp", "seq"),
            P("dp", "seq"),
        ),
        out_specs=P("dp", "seq", None),
        check_vma=False,
    )
```

time: 259 us -> 196 us (0.76)
  the two profiles are of different devices: /device:TPU:25 before, /device:TPU:1 now
where the time goes in v1:
time: 196 us; the launch traced here: 195 us
  blocking collectives  97.8 us (50%)
  waiting for transfers between devices  50.3 us (26%)
  Pallas kernels  17 us (9%)
  between operations  13.5 us (7%)
  matrix products  6.36 us (3%)
  starting transfers between devices  3.71 us (2%)
  local copies, waits for them, and re-layouts  3.22 us (2%)
  other arithmetic  2.87 us (1%)
    all_to_all x1, blocking collectives, local(): lax.all_to_all(sent.reshape(peers, each, depth + 128), 'dp', split_axis=0...  52.1 us
    all_to_all x1, blocking collectives, local(): lax.all_to_all(returned.reshape(peers, each, depth), 'dp', split_axis=0,...  45.7 us
    all_gather x1, waiting for transfers between devices, local(): rows = lax.all_gather(normed, 'seq', axis=0, tiled=True)  34 us
    pallas_call x1, Pallas kernels, heads(): pl.pallas_call(lambda *refs: head_kernel(longest, *refs), grid=(count //...  17 us
    all_gather x1, waiting for transfers between devices, local(): w_full = lax.all_gather(w_output, 'seq', axis=0, tiled=True)  15.6 us
    dot_general x4, matrix products, pick(): lax.dot_general(chosen, rows, (((dim,), (0,)), ((), ())), preferred_eleme...  6.36 us
  transfers between devices with their start and end apart: 3, of which 2 were waited for; matrix products, arithmetic and copies ran while one was open for 0% of the time, Pallas kernels for 9%

profile of v1, /device:TPU:1, one launch (start us, length us, event | category | flops | bytes accessed | tf_op | source)
XLA Modules:
  0.0 194.8 jit_solution(16768736081319814386)
XLA Ops:
  6.5 0.0 all-gather.3.cloned.1.call-start
  6.5 0.9 convert_reduce_fusion.1
  7.5 0.7 multiply_add_fusion
  8.2 0.7 convert_reduce_fusion.3
  8.9 0.1 broadcast_in_dim.10
  9.0 1.4 convolution_convert_fusion
  10.4 0.0 copy-start.5
  10.4 0.1 reshape.37
  10.5 52.1 %all_to_all.15 = bf16[64,4,1152]{2,1,0:T(4,128)(2,1)S(1)} all-to-all(bf16[64,4,1152]{2,1,0:T(4,128)(2,1)S(1)} %reshape.37), channel_id=1, replica_groups=mesh['dp'=64,'seq'=8] {'dp'}, dimensions={0} | all-to-all | bytes 1179648 | tf_op jit(solution)/shard_map/all_to_all | solution.py:141
  62.6 0.1 reshape.38
  62.7 0.0 copy-start.2
  62.8 0.1 convert_reduce_fusion
  62.9 0.0 copy-start.1
  62.9 0.0 copy-start.3
  62.9 0.0 copy-start.4
  62.9 0.1 convert_reduce_fusion.2
  63.1 0.3 fusion.4
  63.4 0.0 copy-done.5
  63.4 1.3 convolution_convert_fusion.3
  64.7 0.0 all-gather.3.cloned.1.call-update
  64.7 0.0 all-gather.5.cloned.1.call-start
  64.7 0.7 all-gather.5.cloned.1.call-update
  65.4 34.0 %all-gather.3.cloned.1.call-done.refs_1_ = bf16[2048,1024]{1,0:T(8,128)(2,1)} async-done(((bf16[256,1024]{1,0:T(8,128)(2,1)}), bf16[2048,1024]{1,0:T(8,128)(2,1)}) %all-gather.3.cloned.1.call-update) | async-done | bytes 4194320 | tf_op jit(solution)/shard_map/all_gather | solution.py:148
  99.4 0.0 copy-done.2
  99.5 0.3 broadcast_in_dim.13.refs_5_
  99.8 0.0 copy-done.1
  99.8 0.0 copy-done.3
  99.8 0.0 copy-done.4
  99.8 0.0 copy-start
  99.8 2.2 %copy-done = bf16[2048,1024]{1,0:T(8,128)(2,1)S(1)} copy-done((bf16[2048,1024]{1,0:T(8,128)(2,1)S(1)}, bf16[2048,1024]{1,0:T(8,128)(2,1)}, u32[]{:S(2)}) %copy-start) | copy-done | bytes 4194328
  102.0 17.0 %shard_map.91 = bf16[2048,128]{1,0:T(8,128)(2,1)} custom-call(f32[1,11]{1,0:T(1,128)S(1)} %copy-done.3, bf16[2048,1024]{1,0:T(8,128)(2,1)S(1)} %copy-done, bf16[1024,512]{1,0:T(8,128)(2,1)S(1)} %copy-done.1, f32[1,128]{1,0:T(1,128)S(1)} %bitcast.20, s32[1,2048]{1,0:T(1,128)S(1)} %copy-done.2, s32[2048,128]{1,0:T(8,128)S(1)} %broadcast_in_dim.13.refs_5_), custom_call_target="tpu_custom_call" | custom-call | tf_op jit(solution)/shard_map/pallas_call | solution.py:91
  119.0 3.7 %all-to-all-start.1 = ((bf16[8,256,128]{2,1,0:T(8,128)(2,1)}), bf16[8,256,128]{2,1,0:T(8,128)(2,1)S(1)}, u32[]{:S(2)}, u32[]{:S(2)}) async-start(bf16[8,256,128]{2,1,0:T(8,128)(2,1)} %bitcast.6), calls=%async_computation.1 | async-start | bytes 1048576 | tf_op jit(solution)/shard_map/all_to_all | solution.py:150
  122.7 15.6 %all-gather.5.cloned.1.call-done = bf16[1024,1024]{1,0:T(8,128)(2,1)} async-done(((bf16[128,1024]{1,0:T(8,128)(2,1)}), bf16[1024,1024]{1,0:T(8,128)(2,1)}) %all-gather.5.cloned.1.call-update) | async-done | bytes 2097168 | tf_op jit(solution)/shard_map/all_gather | solution.py:140
  138.3 0.0 all-to-all-done.1
  138.3 2.5 %convolution_convert_fusion.2 = bf16[256,1024]{1,0:T(8,128)(2,1)S(1)} fusion(bf16[8,256,128]{2,1,0:T(8,128)(2,1)S(1)} %all-to-all-done.1, bf16[8,128,1024]{2,1,0:T(8,128)(2,1)} %bitcast.25, s32[256]{0:T(256)S(1)} %convert_reduce_fusion.2), kind=kOutput, calls=%fused_computation.6 | convolution fusion | flops 671678464 | bytes 3146752 | tf_op jit(solution)/shard_map/dot_general | solution.py:121
  140.8 0.2 reshape.41
  141.0 45.7 %all_to_all.16 = bf16[64,4,1024]{2,1,0:T(4,128)(2,1)S(1)} all-to-all(bf16[64,4,1024]{2,1,0:T(4,128)(2,1)S(1)} %reshape.41), channel_id=1, replica_groups=mesh['dp'=64,'seq'=8] {'dp'}, dimensions={0} | all-to-all | bytes 1048576 | tf_op jit(solution)/shard_map/all_to_all | solution.py:160
  186.7 0.1 reshape.42
  186.8 1.1 fusion.3
  (2 shorter events, 0.0 us)
Async XLA Ops:
  6.5 92.9 %all-gather.3.cloned.1.call-start = ((), (), s32[]{:S(2)}) async-start(), calls=%async_computation.3 | async-start | bytes 4718592 | tf_op jit(solution)/shard_map/all_gather | solution.py:148
  10.4 53.0 %copy-start.5 = (f32[1024]{0:T(1024)S(1)}, f32[1024]{0:T(1024)}, u32[]{:S(2)}) copy-start(f32[1024]{0:T(1024)} %param.13) | copy-start | bytes 12292
  62.7 36.7 %copy-start.2 = (s32[1,2048]{1,0:T(1,128)S(1)}, s32[1,2048]{1,0:T(1,128)}, u32[]{:S(2)}) copy-start(s32[1,2048]{1,0:T(1,128)} %refs_4_.1) | copy-start | bytes 24580
  62.9 36.9 %copy-start.1 = (bf16[1024,512]{1,0:T(8,128)(2,1)S(1)}, bf16[1024,512]{1,0:T(8,128)(2,1)}, u32[]{:S(2)}) copy-start(bf16[1024,512]{1,0:T(8,128)(2,1)} %refs_2_.1) | copy-start | bytes 3145732
  62.9 36.9 %copy-start.3 = (f32[1,11]{1,0:T(1,128)S(1)}, f32[1,11]{1,0:T(1,128)}, u32[]{:S(2)}) copy-start(f32[1,11]{1,0:T(1,128)} %refs_0_.1) | copy-start | bytes 136
  62.9 36.9 %copy-start.4 = (f32[128]{0:T(128)S(1)}, f32[128]{0:T(128)}, u32[]{:S(2)}) copy-start(f32[128]{0:T(128)} %param.14) | copy-start | bytes 1540
  64.7 73.6 %all-gather.5.cloned.1.call-start = ((), (), s32[]{:S(2)}) async-start(), calls=%async_computation.4 | async-start | bytes 2359296 | tf_op jit(solution)/shard_map/all_gather | solution.py:140
  99.8 2.2 %copy-start = (bf16[2048,1024]{1,0:T(8,128)(2,1)S(1)}, bf16[2048,1024]{1,0:T(8,128)(2,1)}, u32[]{:S(2)}) copy-start(bf16[2048,1024]{1,0:T(8,128)(2,1)} %all-gather.3.cloned.1.call-done.refs_1_) | copy-start | bytes 12582916
  119.0 19.2 %all-to-all-start.1 = ((bf16[8,256,128]{2,1,0:T(8,128)(2,1)}), bf16[8,256,128]{2,1,0:T(8,128)(2,1)S(1)}, u32[]{:S(2)}, u32[]{:S(2)}) async-start(bf16[8,256,128]{2,1,0:T(8,128)(2,1)} %bitcast.6), calls=%async_computation.1 | async-start | bytes 1048576 | tf_op jit(solution)/shard_map/all_to_all | solution.py:150
Sparse Core Ops, SparseCore 0:
  64.8 34.5 all-gather.2
  101.6 36.6 all-gather.4

commit v2 on v1

--- a/solution.py
+++ b/solution.py
@@ -1,3 +1,5 @@
+import functools
+
 import jax
 import jax.numpy as jnp
 from jax import lax
@@ -8,6 +10,7 @@
 EPSILON = 1e-05
 BLOCK = 256
 FAR = -1e30
+MESH = pl.DeviceIdType.MESH
 
 
 def norm_rows(values, gain):
@@ -117,6 +120,242 @@
     )
 
 
+def reach_all(barrier, places):
+    for place in places:
+        pl.semaphore_signal(barrier, inc=1, device_id=place, device_id_type=MESH)
+
+
+def dp_exchange(count, start_copy):
+    start_copy(count // 2)
+
+    @pl.loop(1, count // 2)
+    def _(step):
+        start_copy(count // 2 - step)
+        start_copy(count // 2 + step)
+
+
+def enter_kernel(count, sent, shard, got, full, out_sem, in_sem, own_sem, w_out, w_in):
+    me = lax.axis_index("dp")
+    seat = lax.axis_index("seq")
+    seats = lax.axis_size("seq")
+    partner = seat + 1 - 2 * (seat % 2)
+    barrier = pltpu.get_barrier_semaphore()
+
+    @pl.loop(1, count)
+    def _(distance):
+        pl.semaphore_signal(
+            barrier, inc=1, device_id={"dp": (me + distance) % count}, device_id_type=MESH
+        )
+
+    reach_all(barrier, [{"seq": partner}] + [{"seq": (seat + 2 * k) % seats} for k in (1, 2, 3)])
+    pl.semaphore_wait(barrier, count - 1 + 4)
+
+    def row_copy(distance):
+        peer = (me + distance) % count
+        return pltpu.make_async_remote_copy(
+            src_ref=sent.at[peer],
+            dst_ref=got.at[me],
+            send_sem=out_sem.at[distance],
+            recv_sem=in_sem.at[distance],
+            device_id={"dp": peer},
+            device_id_type=MESH,
+        )
+
+    dp_exchange(count, lambda distance: row_copy(distance).start())
+    own = pltpu.make_async_copy(sent.at[me], got.at[me], own_sem.at[0])
+    own.start()
+    own_w = pltpu.make_async_copy(shard, full.at[seat], own_sem.at[1])
+    own_w.start()
+
+    def to_chip(k):
+        return pltpu.make_async_remote_copy(
+            src_ref=shard,
+            dst_ref=full.at[seat],
+            send_sem=w_out.at[k],
+            recv_sem=w_in.at[k],
+            device_id={"seq": (seat + 2 * k) % seats},
+            device_id_type=MESH,
+        )
+
+    def to_partner(k):
+        block = full.at[(seat + seats - 2 * k) % seats]
+        return pltpu.make_async_remote_copy(
+            src_ref=shard if k == 0 else block,
+            dst_ref=block,
+            send_sem=w_out.at[4 + k],
+            recv_sem=w_in.at[4 + k],
+            device_id={"seq": partner},
+            device_id_type=MESH,
+        )
+
+    for k in (1, 2, 3):
+        to_chip(k).start()
+    to_partner(0).start()
+    for k in (1, 3, 2):
+        to_chip(k).wait_recv()
+        to_partner(k).start()
+    for k in (1, 2, 3):
+        to_chip(k).wait_send()
+    for k in range(4):
+        to_partner(k).wait()
+
+    @pl.loop(1, count)
+    def _(distance):
+        row_copy(distance).wait()
+
+    own.wait()
+    own_w.wait()
+
+
+def gather_kernel(block_in, full, ring_out, ring_in, pair_out, pair_in, own_sem):
+    seat = lax.axis_index("seq")
+    seats = lax.axis_size("seq")
+    partner = seat + 1 - 2 * (seat % 2)
+    right, left = (seat + 2) % seats, (seat + seats - 2) % seats
+    across = (seat + 4) % seats
+    half = block_in.shape[0] // 2
+    barrier = pltpu.get_barrier_semaphore()
+    reach_all(barrier, [{"seq": partner}, {"seq": right}, {"seq": left}])
+    pl.semaphore_wait(barrier, 3)
+
+    def piece(ref, part):
+        return ref.at[pl.ds(part * half, half)]
+
+    def ring(slot, source, owner, part, target):
+        return pltpu.make_async_remote_copy(
+            src_ref=piece(source, part),
+            dst_ref=piece(full.at[owner], part),
+            send_sem=ring_out.at[slot],
+            recv_sem=ring_in.at[slot],
+            device_id={"seq": target},
+            device_id_type=MESH,
+        )
+
+    def pair(slot, source, owner, part):
+        return pltpu.make_async_remote_copy(
+            src_ref=piece(source, part),
+            dst_ref=piece(full.at[owner], part),
+            send_sem=pair_out.at[slot],
+            recv_sem=pair_in.at[slot],
+            device_id={"seq": partner},
+            device_id_type=MESH,
+        )
+
+    firsts = [
+        ring(0, block_in, seat, 0, right),
+        ring(1, block_in, seat, 1, left),
+        ring(2, block_in, seat, 1, right),
+        ring(3, block_in, seat, 0, left),
+    ]
+    for copy in firsts:
+        copy.start()
+    own = pltpu.make_async_copy(block_in, full.at[seat], own_sem)
+    own.start()
+    pairs = [pair(0, block_in, seat, 0), pair(1, block_in, seat, 1)]
+    pairs[0].start()
+    pairs[1].start()
+    seconds = [
+        ring(4, full.at[left], left, 0, right),
+        ring(5, full.at[right], right, 1, left),
+    ]
+    arrivals = [(left, 0), (right, 1), (left, 1), (right, 0), (across, 0), (across, 1)]
+    for slot, (owner, part) in enumerate(arrivals):
+        (firsts[slot] if slot < 4 else seconds[slot - 4]).wait_recv()
+        if slot < 2:
+            seconds[slot].start()
+        pairs.append(pair(2 + slot, full.at[owner], owner, part))
+        pairs[-1].start()
+    for copy in firsts + seconds:
+        copy.wait_send()
+    for copy in pairs:
+        copy.wait()
+    own.wait()
+
+
+def swap_kernel(axis, count, sent, got, out_sem, in_sem, own_sem):
+    me = lax.axis_index(axis)
+    barrier = pltpu.get_barrier_semaphore()
+
+    @pl.loop(1, count)
+    def _(distance):
+        pl.semaphore_signal(
+            barrier, inc=1, device_id={axis: (me + distance) % count}, device_id_type=MESH
+        )
+
+    pl.semaphore_wait(barrier, count - 1)
+
+    def copy(distance):
+        peer = (me + distance) % count
+        return pltpu.make_async_remote_copy(
+            src_ref=sent.at[peer],
+            dst_ref=got.at[me],
+            send_sem=out_sem.at[distance],
+            recv_sem=in_sem.at[distance],
+            device_id={axis: peer},
+            device_id_type=MESH,
+        )
+
+    dp_exchange(count, lambda distance: copy(distance).start())
+    own = pltpu.make_async_copy(sent.at[me], got.at[me], own_sem)
+    own.start()
+
+    @pl.loop(1, count)
+    def _(distance):
+        copy(distance).wait()
+
+    own.wait()
+
+
+IN_VMEM = pl.BlockSpec(memory_space=pltpu.VMEM)
+DMA = pltpu.SemaphoreType.DMA
+
+
+def remote(kernel, number, operands, shapes, scratch):
+    return pl.pallas_call(
+        kernel,
+        out_shape=tuple(jax.ShapeDtypeStruct(shape, jnp.bfloat16) for shape in shapes),
+        in_specs=[IN_VMEM] * len(operands),
+        out_specs=(IN_VMEM,) * len(shapes),
+        scratch_shapes=scratch,
+        compiler_params=pltpu.CompilerParams(
+            collective_id=number, has_side_effects=True, vmem_limit_bytes=32 << 20
+        ),
+    )(*operands)
+
+
+def enter(sent, shard):
+    count, seats = lax.axis_size("dp"), lax.axis_size("seq")
+    return remote(
+        functools.partial(enter_kernel, count),
+        0,
+        (sent, shard),
+        (sent.shape, (seats,) + shard.shape),
+        [DMA((count,)), DMA((count,)), DMA((2,)), DMA((8,)), DMA((8,))],
+    )
+
+
+def gather(block):
+    seats = lax.axis_size("seq")
+    return remote(
+        gather_kernel,
+        1,
+        (block,),
+        ((seats,) + block.shape,),
+        [DMA((6,)), DMA((6,)), DMA((8,)), DMA((8,)), DMA(())],
+    )[0]
+
+
+def swap(sent, axis, number):
+    count = lax.axis_size(axis)
+    return remote(
+        functools.partial(swap_kernel, axis, count),
+        number,
+        (sent,),
+        (sent.shape,),
+        [DMA((count,)), DMA((count,)), DMA(())],
+    )[0]
+
+
 def pick(chosen, rows, dim):
     return lax.dot_general(
         chosen, rows, (((dim,), (0,)), ((), ())), preferred_element_type=jnp.float32
@@ -137,29 +376,23 @@
         [events[0], jnp.broadcast_to(owner_row[0][:, None], (count, 128)).astype(jnp.bfloat16)], axis=1
     )
     sent = pick(to_slot, tagged, 1)
-    w_full = lax.all_gather(w_output, "seq", axis=0, tiled=True)
-    got = lax.all_to_all(
-        sent.reshape(peers, each, depth + 128), "dp", split_axis=0, concat_axis=0, tiled=True
-    ).reshape(count, depth + 128)
+    got, w_full = enter(sent.reshape(peers, each, depth + 128), w_output)
+    got = got.reshape(count, depth + 128)
     place = got[:, depth].astype(jnp.int32)
     to_place = (place[:, None] == index[None, :]).astype(jnp.bfloat16)
     normed = norm_rows(got[:, :depth].astype(jnp.float32), in_gain).astype(jnp.bfloat16)
     normed = pick(to_place, normed, 0)
-    rows = lax.all_gather(normed, "seq", axis=0, tiled=True)
+    rows = gather(normed).reshape(parts * count, depth)
     gated = heads(rows, w_project, rel_bias, out_gain, user_ids, count * parts // 2)
-    mine = lax.all_to_all(
-        gated.reshape(parts, count, -1), "seq", split_axis=0, concat_axis=0, tiled=True
-    )
+    mine = swap(gated.reshape(parts, count, -1), "seq", 2)
     merged = jnp.einsum(
         "hrd,hdo->ro",
         mine,
-        w_full.reshape(parts, -1, depth),
+        w_full,
         preferred_element_type=jnp.float32,
     ).astype(jnp.bfloat16)
     returned = pick(to_place, merged, 1)
-    home = lax.all_to_all(
-        returned.reshape(peers, each, depth), "dp", split_axis=0, concat_axis=0, tiled=True
-    ).reshape(count, depth)
+    home = swap(returned.reshape(peers, each, depth), "dp", 3).reshape(count, depth)
     return pick(to_slot, home, 0)[None]
 
 

time: 196 us -> 141 us (0.72)
  Pallas kernels: 17 us -> 131 us
  blocking collectives: 97.8 us -> 0 us
  waiting for transfers between devices: 50.3 us -> 0 us
  between operations: 13.5 us -> 0.21 us
  starting transfers between devices: 3.71 us -> 0 us
  matrix products: 6.36 us -> 3.97 us
    pallas_call x0 -> x4, Pallas kernels: none -> 115 us  [remote(): pl.pallas_call(kernel, out_shape=tuple((jax.ShapeDtypeStruct(shape, jnp.b...]
    all_to_all x2 -> x0, blocking collectives: 97.8 us -> none  [the longest x1 52.1 us: local(): lax.all_to_all(sent.reshape(peers, each, depth + 128), 'dp', split_axis=0...]
    all_gather x2 -> x0, waiting for transfers between devices: 49.6 us -> none  [the longest x1 34 us: local(): rows = lax.all_gather(normed, 'seq', axis=0, tiled=True)]
    all_to_all x1 -> x0, starting transfers between devices: 3.67 us -> none  [local(): lax.all_to_all(gated.reshape(parts, count, -1), 'seq', split_axis=0, conc...]
    dot_general x4, matrix products: 6.36 us -> 3.97 us  [pick(): lax.dot_general(chosen, rows, (((dim,), (0,)), ((), ())), preferred_eleme...]
  transfers between devices with their start and end apart: 3 -> 0, of which waited for: 2 -> 0; matrix products, arithmetic and copies ran while one was open for 0% -> 0% of each run, Pallas kernels for 9% -> 0%
where the time goes in v2:
time: 141 us
  Pallas kernels  131 us (93%)
  matrix products  3.97 us (3%)
  other arithmetic  2.83 us (2%)
  local copies, waits for them, and re-layouts  2.47 us (2%)
    pallas_call x4, Pallas kernels, remote(): pl.pallas_call(kernel, out_shape=tuple((jax.ShapeDtypeStruct(shape, jnp.b...  115 us
    pallas_call x1, Pallas kernels, heads(): pl.pallas_call(lambda *refs: head_kernel(longest, *refs), grid=(count //...  16.4 us
    dot_general x4, matrix products, pick(): lax.dot_general(chosen, rows, (((dim,), (0,)), ((), ())), preferred_eleme...  3.97 us

profile of v2, /device:TPU:1, one launch (start us, length us, event | category | flops | bytes accessed | tf_op | source)
XLA Modules:
  0.0 141.0 jit_solution(7274215115566596550)
XLA Ops:
  0.0 0.0 copy-start.2
  0.0 0.0 copy-start.1
  0.0 0.7 convert_reduce_fusion.2
  0.7 0.9 convert_reduce_fusion.1
  1.7 0.7 multiply_add_fusion
  2.4 0.1 broadcast_in_dim.10
  2.5 1.4 convolution_convert_fusion
  3.9 0.1 reshape.37.sent
  4.0 0.0 copy-done.2
  4.0 0.0 copy-start.7
  4.0 0.3 broadcast_in_dim.13.refs_5_
  4.4 0.0 copy-done.1
  4.4 47.0 %shard_map.91 = (bf16[64,4,1152]{2,1,0:T(4,128)(2,1)S(1)}, bf16[8,128,1024]{2,1,0:T(8,128)(2,1)S(1)}) custom-call(bf16[64,4,1152]{2,1,0:T(4,128)(2,1)S(1)} %reshape.37.sent, bf16[128,1024]{1,0:T(8,128)(2,1)S(1)} %copy-done.1), custom_call_target="tpu_custom_call" | custom-call | tf_op jit(solution)/shard_map/pallas_call | solution.py:314
  51.4 0.0 copy-start.5
  51.4 1.3 copy-done.5
  52.7 0.1 reshape.38
  52.9 0.1 convert_reduce_fusion
  53.0 0.3 fusion.4
  53.3 0.1 copy.13
  53.4 0.0 copy-done.7
  53.4 0.5 convolution_convert_fusion.3.block_in
  53.9 0.0 copy-start
  53.9 0.0 copy-start.3
  54.0 0.0 copy-start.4
  54.0 24.4 %shard_map.92 = bf16[8,256,1024]{2,1,0:T(8,128)(2,1)S(1)} custom-call(bf16[256,1024]{1,0:T(8,128)(2,1)S(1)} %convolution_convert_fusion.3.block_in), custom_call_target="tpu_custom_call" | custom-call | tf_op jit(solution)/shard_map/pallas_call | solution.py:314
  78.4 0.0 copy-done
  78.4 0.0 copy-done.3
  78.4 0.0 copy-done.4
  78.4 0.0 copy-start.6
  78.5 16.4 %shard_map.93 = bf16[2048,128]{1,0:T(8,128)(2,1)S(1)} custom-call(f32[1,11]{1,0:T(1,128)S(1)} %copy-done.3, bf16[2048,1024]{1,0:T(8,128)(2,1)S(1)} %bitcast.20, bf16[1024,512]{1,0:T(8,128)(2,1)S(1)} %copy-done, f32[1,128]{1,0:T(1,128)S(1)} %bitcast.23, s32[1,2048]{1,0:T(1,128)S(1)} %copy-done.2, s32[2048,128]{1,0:T(8,128)S(1)} %broadcast_in_dim.13.refs_5_), custom_call_target="tpu_custom_call" | custom-call | tf_op jit(solution)/shard_map/pallas_call | solution.py:94
  94.8 10.0 %shard_map.94 = bf16[8,256,128]{2,1,0:T(8,128)(2,1)S(1)} custom-call(bf16[8,256,128]{2,1,0:T(8,128)(2,1)S(1)} %bitcast.21), custom_call_target="tpu_custom_call" | custom-call | tf_op jit(solution)/shard_map/pallas_call | solution.py:314
  104.8 0.0 copy-done.6
  104.8 0.9 convolution_convert_fusion.2
  105.7 0.2 reshape.41.sent
  106.0 33.7 %shard_map.95 = bf16[64,4,1024]{2,1,0:T(4,128)(2,1)S(1)} custom-call(bf16[64,4,1024]{2,1,0:T(4,128)(2,1)S(1)} %reshape.41.sent), custom_call_target="tpu_custom_call" | custom-call | tf_op jit(solution)/shard_map/pallas_call | solution.py:314
  139.7 0.1 reshape.42
  139.8 1.1 fusion.3
  (3 shorter events, 0.0 us)
Async XLA Ops:
  0.0 4.0 %copy-start.2 = (s32[1,2048]{1,0:T(1,128)S(1)}, s32[1,2048]{1,0:T(1,128)}, u32[]{:S(2)}) copy-start(s32[1,2048]{1,0:T(1,128)} %refs_4_.1) | copy-start | bytes 24580
  0.0 4.4 %copy-start.1 = (bf16[128,1024]{1,0:T(8,128)(2,1)S(1)}, bf16[128,1024]{1,0:T(8,128)(2,1)}, u32[]{:S(2)}) copy-start(bf16[128,1024]{1,0:T(8,128)(2,1)} %shard.1) | copy-start | bytes 786436
  4.0 49.4 %copy-start.7 = (f32[1024]{0:T(1024)S(1)}, f32[1024]{0:T(1024)}, u32[]{:S(2)}) copy-start(f32[1024]{0:T(1024)} %param.13) | copy-start | bytes 12292
  51.4 1.4 copy-start.5
  53.9 24.5 %copy-start = (bf16[1024,512]{1,0:T(8,128)(2,1)S(1)}, bf16[1024,512]{1,0:T(8,128)(2,1)}, u32[]{:S(2)}) copy-start(bf16[1024,512]{1,0:T(8,128)(2,1)} %refs_2_.1) | copy-start | bytes 3145732
  53.9 24.5 %copy-start.3 = (f32[1,11]{1,0:T(1,128)S(1)}, f32[1,11]{1,0:T(1,128)}, u32[]{:S(2)}) copy-start(f32[1,11]{1,0:T(1,128)} %refs_0_.1) | copy-start | bytes 136
  54.0 24.5 %copy-start.4 = (f32[128]{0:T(128)S(1)}, f32[128]{0:T(128)}, u32[]{:S(2)}) copy-start(f32[128]{0:T(128)} %param.14) | copy-start | bytes 1540
  78.4 26.4 %copy-start.6 = (bf16[8,128,1024]{2,1,0:T(8,128)(2,1)S(1)}, bf16[8,128,1024]{2,1,0:T(8,128)(2,1)}, u32[]{:S(2)}) copy-start(bf16[8,128,1024]{2,1,0:T(8,128)(2,1)} %copy-done.5) | copy-start | bytes 6291460

commit v3 on v2

--- a/solution.py
+++ b/solution.py
@@ -44,82 +44,6 @@
     return total
 
 
-def head_kernel(longest, table, x_ref, w_ref, gain_ref, row_ids, col_ids, out_ref, proj, bias, acc):
-    step = pl.program_id(0)
-    reach = bias.shape[0]
-    width = acc.shape[1]
-
-    @pl.when(step == 0)
-    def _():
-        for offset in range(reach):
-            bias[offset] = half_bias(table, offset, longest, table.shape[1])
-
-    here = pl.ds(pl.multiple_of(step * BLOCK, BLOCK), BLOCK)
-    proj[here, :] = half_silu(
-        0.5 * jnp.dot(x_ref[...], w_ref[...], preferred_element_type=jnp.float32)
-    ).astype(jnp.bfloat16)
-    ids = jnp.concatenate([col_ids[...]] * (BLOCK // col_ids.shape[1]), axis=1)
-    scale = 0.5 * width ** (-0.5)
-
-    def term(offset):
-        first = pl.multiple_of((step - offset) * BLOCK, BLOCK)
-        there = pl.ds(first, BLOCK)
-        scores = lax.dot_general(
-            proj[here, :width],
-            proj[there, width : 2 * width],
-            (((1,), (1,)), ((), ())),
-            preferred_element_type=jnp.float32,
-        )
-        weights = half_silu(scores * scale + bias[offset])
-        weights = jnp.where(ids == row_ids[:, there], weights, 0.0).astype(jnp.bfloat16)
-        return jnp.dot(
-            weights, proj[there, 2 * width : 3 * width], preferred_element_type=jnp.float32
-        )
-
-    acc[...] = term(0)
-    for offset in range(1, reach):
-
-        @pl.when(step >= offset)
-        def _(offset=offset):
-            acc[...] += term(offset)
-
-    gate = proj[here, 3 * width :].astype(jnp.float32)
-    out_ref[...] = (norm_rows(acc[...], gain_ref[...]) * gate).astype(jnp.bfloat16)
-
-
-def heads(rows, w_project, table, gain, segment, longest):
-    count, depth = rows.shape
-    width = gain.shape[0]
-    reach = longest // BLOCK + 1
-    return pl.pallas_call(
-        lambda *refs: head_kernel(longest, *refs),
-        grid=(count // BLOCK,),
-        out_shape=jax.ShapeDtypeStruct((count, width), jnp.bfloat16),
-        in_specs=[
-            pl.BlockSpec(memory_space=pltpu.SMEM),
-            pl.BlockSpec((BLOCK, depth), lambda i: (i, 0)),
-            pl.BlockSpec((depth, 4 * width), lambda i: (0, 0)),
-            pl.BlockSpec((1, width), lambda i: (0, 0)),
-            pl.BlockSpec((1, count), lambda i: (0, 0)),
-            pl.BlockSpec((BLOCK, 128), lambda i: (i, 0)),
-        ],
-        out_specs=pl.BlockSpec((BLOCK, width), lambda i: (i, 0)),
-        scratch_shapes=[
-            pltpu.VMEM((count, 4 * width), jnp.bfloat16),
-            pltpu.VMEM((reach, BLOCK, BLOCK), jnp.float32),
-            pltpu.VMEM((BLOCK, width), jnp.float32),
-        ],
-        compiler_params=pltpu.CompilerParams(vmem_limit_bytes=32 << 20),
-    )(
-        table,
-        rows,
-        w_project,
-        gain[None],
-        segment,
-        jnp.broadcast_to(segment.reshape(count, 1), (count, 128)),
-    )
-
-
 def reach_all(barrier, places):
     for place in places:
         pl.semaphore_signal(barrier, inc=1, device_id=place, device_id_type=MESH)
@@ -207,13 +131,14 @@
     own_w.wait()
 
 
-def gather_kernel(block_in, full, ring_out, ring_in, pair_out, pair_in, own_sem):
+def gather_kernel(block_in, w_ref, proj, full, ring_out, ring_in, pair_out, pair_in):
     seat = lax.axis_index("seq")
     seats = lax.axis_size("seq")
     partner = seat + 1 - 2 * (seat % 2)
     right, left = (seat + 2) % seats, (seat + seats - 2) % seats
     across = (seat + 4) % seats
-    half = block_in.shape[0] // 2
+    rows = block_in.shape[0]
+    half = rows // 2
     barrier = pltpu.get_barrier_semaphore()
     reach_all(barrier, [{"seq": partner}, {"seq": right}, {"seq": left}])
     pl.semaphore_wait(barrier, 3)
@@ -249,8 +174,6 @@
     ]
     for copy in firsts:
         copy.start()
-    own = pltpu.make_async_copy(block_in, full.at[seat], own_sem)
-    own.start()
     pairs = [pair(0, block_in, seat, 0), pair(1, block_in, seat, 1)]
     pairs[0].start()
     pairs[1].start()
@@ -258,6 +181,17 @@
         ring(4, full.at[left], left, 0, right),
         ring(5, full.at[right], right, 1, left),
     ]
+
+    def project(block, owner):
+        there = pl.ds(pl.multiple_of(owner * rows, rows), rows)
+        proj[there, :] = half_silu(
+            0.5 * jnp.dot(block[...], w_ref[...], preferred_element_type=jnp.float32)
+        ).astype(jnp.bfloat16)
+
+    project(block_in, seat)
+    pairs[0].wait_recv()
+    pairs[1].wait_recv()
+    project(full.at[partner], partner)
     arrivals = [(left, 0), (right, 1), (left, 1), (right, 0), (across, 0), (across, 1)]
     for slot, (owner, part) in enumerate(arrivals):
         (firsts[slot] if slot < 4 else seconds[slot - 4]).wait_recv()
@@ -265,43 +199,123 @@
             seconds[slot].start()
         pairs.append(pair(2 + slot, full.at[owner], owner, part))
         pairs[-1].start()
-    for copy in firsts + seconds:
+        if slot == 3:
+            project(full.at[left], left)
+            project(full.at[right], right)
+            for early in (2, 3, 4, 5):
+                pairs[early].wait_recv()
+            for owner in (left, right):
+                other = owner + 1 - 2 * (owner % 2)
+                project(full.at[other], other)
+    project(full.at[across], across)
+    pairs[6].wait_recv()
+    pairs[7].wait_recv()
+    other = across + 1 - 2 * (across % 2)
+    project(full.at[other], other)
+    for copy in firsts + seconds + pairs:
         copy.wait_send()
-    for copy in pairs:
-        copy.wait()
-    own.wait()
-
-
-def swap_kernel(axis, count, sent, got, out_sem, in_sem, own_sem):
-    me = lax.axis_index(axis)
+
+
+def tail_kernel(
+    longest, peers, table, proj, gain_ref, row_ids, col_ids, w_full, to_place, home,
+    bias, acc, gated, mine, returned, swap_out, swap_in, back_out, back_in, own_sem,
+):
+    me = lax.axis_index("dp")
+    seat = lax.axis_index("seq")
+    seats = lax.axis_size("seq")
+    reach = bias.shape[0]
+    width = acc.shape[1]
     barrier = pltpu.get_barrier_semaphore()
 
-    @pl.loop(1, count)
+    @pl.loop(1, peers)
     def _(distance):
         pl.semaphore_signal(
-            barrier, inc=1, device_id={axis: (me + distance) % count}, device_id_type=MESH
-        )
-
-    pl.semaphore_wait(barrier, count - 1)
-
-    def copy(distance):
-        peer = (me + distance) % count
-        return pltpu.make_async_remote_copy(
-            src_ref=sent.at[peer],
-            dst_ref=got.at[me],
-            send_sem=out_sem.at[distance],
-            recv_sem=in_sem.at[distance],
-            device_id={axis: peer},
-            device_id_type=MESH,
-        )
-
-    dp_exchange(count, lambda distance: copy(distance).start())
-    own = pltpu.make_async_copy(sent.at[me], got.at[me], own_sem)
+            barrier, inc=1, device_id={"dp": (me + distance) % peers}, device_id_type=MESH
+        )
+
+    reach_all(barrier, [{"seq": (seat + k) % seats} for k in range(1, seats)])
+
+    for offset in range(reach):
+        bias[offset] = half_bias(table, offset, longest, table.shape[1])
+    scale = 0.5 * width ** (-0.5)
+
+    def swap(distance):
+        return pltpu.make_async_remote_copy(
+            src_ref=gated.at[(seat + distance) % seats],
+            dst_ref=mine.at[seat],
+            send_sem=swap_out.at[distance],
+            recv_sem=swap_in.at[distance],
+            device_id={"seq": (seat + distance) % seats},
+            device_id_type=MESH,
+        )
+
+    @pl.loop(1, seats + 1)
+    def _(distance):
+        block = (seat + distance) % seats
+        here = pl.ds(pl.multiple_of(block * BLOCK, BLOCK), BLOCK)
+        ids = jnp.concatenate([col_ids[here, :]] * (BLOCK // col_ids.shape[1]), axis=1)
+
+        def term(offset):
+            there = pl.ds(pl.multiple_of((block - offset) * BLOCK, BLOCK), BLOCK)
+            scores = lax.dot_general(
+                proj[here, :width],
+                proj[there, width : 2 * width],
+                (((1,), (1,)), ((), ())),
+                preferred_element_type=jnp.float32,
+            )
+            weights = half_silu(scores * scale + bias[offset])
+            weights = jnp.where(ids == row_ids[:, there], weights, 0.0).astype(jnp.bfloat16)
+            return jnp.dot(
+                weights, proj[there, 2 * width : 3 * width], preferred_element_type=jnp.float32
+            )
+
+        acc[...] = term(0)
+
+        @pl.when(distance == 2)
+        def _():
+            pl.semaphore_wait(barrier, peers - 1 + seats - 1)
+
+        @pl.when(distance >= 2)
+        def _():
+            swap(distance - 1).start()
+
+        for offset in range(1, reach):
+
+            @pl.when(block >= offset)
+            def _(offset=offset):
+                acc[...] += term(offset)
+
+        gate = proj[here, 3 * width :].astype(jnp.float32)
+        gated[block] = (norm_rows(acc[...], gain_ref[...]) * gate).astype(jnp.bfloat16)
+
+    mine[seat] = gated[seat]
+    for distance in range(1, seats):
+        swap(distance).wait_recv()
+    rows = jnp.concatenate([mine[head] for head in range(seats)], axis=1)
+    merged = jnp.dot(rows, w_full[...], preferred_element_type=jnp.float32).astype(jnp.bfloat16)
+    picked = jnp.dot(to_place[...], merged, preferred_element_type=jnp.float32)
+    returned[...] = picked.reshape(returned.shape).astype(jnp.bfloat16)
+    for distance in range(1, seats):
+        swap(distance).wait_send()
+
+    def back(distance):
+        peer = (me + distance) % peers
+        return pltpu.make_async_remote_copy(
+            src_ref=returned.at[peer],
+            dst_ref=home.at[me],
+            send_sem=back_out.at[distance],
+            recv_sem=back_in.at[distance],
+            device_id={"dp": peer},
+            device_id_type=MESH,
+        )
+
+    dp_exchange(peers, lambda distance: back(distance).start())
+    own = pltpu.make_async_copy(returned.at[me], home.at[me], own_sem)
     own.start()
 
-    @pl.loop(1, count)
+    @pl.loop(1, peers)
     def _(distance):
-        copy(distance).wait()
+        back(distance).wait()
 
     own.wait()
 
@@ -334,26 +348,52 @@
     )
 
 
-def gather(block):
+def gather(block, w_project):
     seats = lax.axis_size("seq")
+    rows, depth = block.shape
     return remote(
         gather_kernel,
         1,
-        (block,),
-        ((seats,) + block.shape,),
-        [DMA((6,)), DMA((6,)), DMA((8,)), DMA((8,)), DMA(())],
+        (block, w_project),
+        ((seats * rows, w_project.shape[1]),),
+        [pltpu.VMEM((seats, rows, depth), jnp.bfloat16), DMA((6,)), DMA((6,)), DMA((8,)), DMA((8,))],
     )[0]
 
 
-def swap(sent, axis, number):
-    count = lax.axis_size(axis)
-    return remote(
-        functools.partial(swap_kernel, axis, count),
-        number,
-        (sent,),
-        (sent.shape,),
-        [DMA((count,)), DMA((count,)), DMA(())],
-    )[0]
+def tail(proj, table, gain, segment, w_full, to_place):
+    peers, seats = lax.axis_size("dp"), lax.axis_size("seq")
+    count, (width,), depth = proj.shape[0], gain.shape, w_full.shape[1]
+    rows = to_place.shape[0]
+    reach = count // 2 // BLOCK + 1
+    return pl.pallas_call(
+        functools.partial(tail_kernel, count // 2, peers),
+        out_shape=jax.ShapeDtypeStruct((peers, rows // peers, depth), jnp.bfloat16),
+        in_specs=[pl.BlockSpec(memory_space=pltpu.SMEM)] + [IN_VMEM] * 6,
+        out_specs=IN_VMEM,
+        scratch_shapes=[
+            pltpu.VMEM((reach, BLOCK, BLOCK), jnp.float32),
+            pltpu.VMEM((BLOCK, width), jnp.float32),
+            pltpu.VMEM((seats, rows, width), jnp.bfloat16),
+            pltpu.VMEM((seats, rows, width), jnp.bfloat16),
+            pltpu.VMEM((peers, rows // peers, depth), jnp.bfloat16),
+            DMA((seats,)),
+            DMA((seats,)),
+            DMA((peers,)),
+            DMA((peers,)),
+            DMA(()),
+        ],
+        compiler_params=pltpu.CompilerParams(
+            collective_id=2, has_side_effects=True, vmem_limit_bytes=32 << 20
+        ),
+    )(
+        table,
+        proj,
+        gain[None],
+        segment,
+        jnp.broadcast_to(segment.reshape(count, 1), (count, 128)),
+        w_full,
+        to_place,
+    )
 
 
 def pick(chosen, rows, dim):
@@ -364,7 +404,6 @@
 
 def local(events, w_project, w_output, rel_bias, in_gain, out_gain, user_ids, owner_dev, owner_row):
     peers = lax.axis_size("dp")
-    parts = lax.axis_size("seq")
     count, depth = events.shape[1:]
     each = count // peers
     owners = owner_dev[0]
@@ -382,17 +421,9 @@
     to_place = (place[:, None] == index[None, :]).astype(jnp.bfloat16)
     normed = norm_rows(got[:, :depth].astype(jnp.float32), in_gain).astype(jnp.bfloat16)
     normed = pick(to_place, normed, 0)
-    rows = gather(normed).reshape(parts * count, depth)
-    gated = heads(rows, w_project, rel_bias, out_gain, user_ids, count * parts // 2)
-    mine = swap(gated.reshape(parts, count, -1), "seq", 2)
-    merged = jnp.einsum(
-        "hrd,hdo->ro",
-        mine,
-        w_full,
-        preferred_element_type=jnp.float32,
-    ).astype(jnp.bfloat16)
-    returned = pick(to_place, merged, 1)
-    home = swap(returned.reshape(peers, each, depth), "dp", 3).reshape(count, depth)
+    proj = gather(normed, w_project)
+    home = tail(proj, rel_bias, out_gain, user_ids, w_full.reshape(-1, depth), to_place)
+    home = home.reshape(count, depth)
     return pick(to_slot, home, 0)[None]
 
 

time: 141 us -> 131 us (0.929)
  Pallas kernels: 131 us -> 121 us
    pallas_call x4 -> x2, Pallas kernels: 115 us -> 71.9 us  [remote(): pl.pallas_call(kernel, out_shape=tuple((jax.ShapeDtypeStruct(shape, jnp.b...]
    pallas_call x1, Pallas kernels: 16.4 us -> 49.1 us  [tail(): pl.pallas_call(functools.partial(tail_kernel, count // 2, peers), out_sha...]
    dot_general x4 -> x3, matrix products: 3.97 us -> 3.05 us  [pick(): lax.dot_general(chosen, rows, (((dim,), (0,)), ((), ())), preferred_eleme...]
where the time goes in v3:
time: 131 us; the launch traced here: 130 us
  Pallas kernels  121 us (92%)
  local copies, waits for them, and re-layouts  3.18 us (2%)
  matrix products  3.05 us (2%)
  other arithmetic  2.88 us (2%)
    pallas_call x2, Pallas kernels, remote(): pl.pallas_call(kernel, out_shape=tuple((jax.ShapeDtypeStruct(shape, jnp.b...  71.9 us
    pallas_call x1, Pallas kernels, tail(): pl.pallas_call(functools.partial(tail_kernel, count // 2, peers), out_sha...  49.1 us
    dot_general x3, matrix products, pick(): lax.dot_general(chosen, rows, (((dim,), (0,)), ((), ())), preferred_eleme...  3.05 us

profile of v3, /device:TPU:1, one launch (start us, length us, event | category | flops | bytes accessed | tf_op | source)
XLA Modules:
  0.0 130.3 jit_solution(14571146165267219028)
XLA Ops:
  0.0 0.7 convert_reduce_fusion.2
  0.7 0.9 convert_reduce_fusion.1
  1.6 0.7 multiply_add_fusion
  2.3 0.1 broadcast_in_dim.10
  2.4 0.0 copy-start.4
  2.4 1.4 %convolution_convert_fusion = bf16[256,1152]{1,0:T(8,128)(2,1)S(1)} fusion(bf16[256,128]{1,0:T(8,128)(2,1)S(1)} %broadcast_in_dim.10, bf16[256,1024]{1,0:T(8,128)(2,1)} %bitcast.20, s32[256]{0:T(256)S(1)} %bitcast.17), kind=kOutput, calls=%fused_computation | convolution fusion | flops 152535040 | bytes 1180672 | tf_op jit(solution)/shard_map/dot_general | solution.py:400
  3.8 0.0 copy-start.3
  3.8 0.1 reshape.31.sent
  4.0 0.0 copy-done.4
  4.0 0.3 broadcast_in_dim.13.col_ids
  4.3 0.5 copy-done.3
  4.8 47.0 %shard_map.91 = (bf16[64,4,1152]{2,1,0:T(4,128)(2,1)S(1)}, bf16[8,128,1024]{2,1,0:T(8,128)(2,1)S(1)}) custom-call(bf16[64,4,1152]{2,1,0:T(4,128)(2,1)S(1)} %reshape.31.sent, bf16[128,1024]{1,0:T(8,128)(2,1)S(1)} %copy-done.3), custom_call_target="tpu_custom_call" | custom-call | tf_op jit(solution)/shard_map/pallas_call | solution.py:328
  51.8 0.0 copy-start
  51.8 1.3 %copy-done = bf16[8,128,1024]{2,1,0:T(8,128)(2,1)} copy-done((bf16[8,128,1024]{2,1,0:T(8,128)(2,1)}, bf16[8,128,1024]{2,1,0:T(8,128)(2,1)S(1)}, u32[]{:S(2)}) %copy-start) | copy-done | bytes 2097176
  53.1 0.0 copy-start.7
  53.1 0.1 reshape.32
  53.3 0.1 convert_reduce_fusion
  53.4 0.3 fusion.3
  53.7 0.0 copy-start.2
  53.7 0.1 copy.13
  53.8 0.0 copy-done.7
  53.8 0.5 convolution_convert_fusion.2.block_in
  54.3 0.1 fusion.14.to_place
  54.5 0.5 copy-done.2
  54.9 0.0 copy-start.1
  54.9 0.0 copy-start.5
  54.9 0.0 copy-start.6
  54.9 24.9 %shard_map.92.proj = bf16[2048,512]{1,0:T(8,128)(2,1)S(1)} custom-call(bf16[256,1024]{1,0:T(8,128)(2,1)S(1)} %convolution_convert_fusion.2.block_in, bf16[1024,512]{1,0:T(8,128)(2,1)S(1)} %copy-done.2), custom_call_target="tpu_custom_call" | custom-call | tf_op jit(solution)/shard_map/pallas_call | solution.py:328
  79.8 0.0 copy-done.1
  79.8 0.0 copy-done.5
  79.9 0.0 copy-done.6
  79.9 49.1 %shard_map.93 = bf16[64,4,1024]{2,1,0:T(4,128)(2,1)S(1)} custom-call(f32[1,11]{1,0:T(1,128)S(1)} %copy-done.5, bf16[2048,512]{1,0:T(8,128)(2,1)S(1)} %shard_map.92.proj, f32[1,128]{1,0:T(1,128)S(1)} %bitcast.13, s32[1,2048]{1,0:T(1,128)S(1)} %copy-done.4, s32[2048,128]{1,0:T(8,128)S(1)} %broadcast_in_dim.13.col_ids, bf16[1024,1024]{1,0:T(8,128)(2,1)S(1)} %bitcast.11, ...), custom_call_target="tpu_custom_call" | custom-call | tf_op jit(solution)/shard_map/pallas_call | solution.py:368
  129.0 0.1 reshape.34
  129.1 1.1 fusion.2
  (3 shorter events, 0.0 us)
Async XLA Ops:
  2.4 1.6 %copy-start.4 = (s32[1,2048]{1,0:T(1,128)S(1)}, s32[1,2048]{1,0:T(1,128)}, u32[]{:S(2)}) copy-start(s32[1,2048]{1,0:T(1,128)} %row_ids.1) | copy-start | bytes 24580
  3.8 1.0 copy-start.3
  51.8 1.4 %copy-start = (bf16[8,128,1024]{2,1,0:T(8,128)(2,1)}, bf16[8,128,1024]{2,1,0:T(8,128)(2,1)S(1)}, u32[]{:S(2)}) copy-start(bf16[8,128,1024]{2,1,0:T(8,128)(2,1)S(1)} %get-tuple-element.8) | copy-start | bytes 6291460
  53.1 0.7 copy-start.7
  53.7 1.2 copy-start.2
  54.9 24.9 %copy-start.1 = (bf16[8,128,1024]{2,1,0:T(8,128)(2,1)S(1)}, bf16[8,128,1024]{2,1,0:T(8,128)(2,1)}, u32[]{:S(2)}) copy-start(bf16[8,128,1024]{2,1,0:T(8,128)(2,1)} %copy-done) | copy-start | bytes 6291460
  54.9 24.9 %copy-start.5 = (f32[1,11]{1,0:T(1,128)S(1)}, f32[1,11]{1,0:T(1,128)}, u32[]{:S(2)}) copy-start(f32[1,11]{1,0:T(1,128)} %table.1) | copy-start | bytes 136
  54.9 24.9 %copy-start.6 = (f32[128]{0:T(128)S(1)}, f32[128]{0:T(128)}, u32[]{:S(2)}) copy-start(f32[128]{0:T(128)} %param.14) | copy-start | bytes 1540

commit v4 on v3

--- a/solution.py
+++ b/solution.py
@@ -49,20 +49,22 @@
         pl.semaphore_signal(barrier, inc=1, device_id=place, device_id_type=MESH)
 
 
-def dp_exchange(count, start_copy):
-    start_copy(count // 2)
-
-    @pl.loop(1, count // 2)
-    def _(step):
-        start_copy(count // 2 - step)
-        start_copy(count // 2 + step)
-
-
-def enter_kernel(count, sent, shard, got, full, out_sem, in_sem, own_sem, w_out, w_in):
+def far_first(turn, count):
+    return count // 2 - (turn + 1) // 2 * (2 * (turn % 2) - 1)
+
+
+def enter_kernel(
+    count, quarters, sent, shard, gain, w_ref, full_w, proj, to_place,
+    got, full, mixed, out_sem, in_sem, w_out, w_in, ring_out, ring_in, pair_out, pair_in, own_sem,
+):
     me = lax.axis_index("dp")
     seat = lax.axis_index("seq")
     seats = lax.axis_size("seq")
     partner = seat + 1 - 2 * (seat % 2)
+    right, left, across = (seat + 2) % seats, (seat + seats - 2) % seats, (seat + 4) % seats
+    turns = count // quarters
+    rows = full.shape[2]
+    depth = gain.shape[1]
     barrier = pltpu.get_barrier_semaphore()
 
     @pl.loop(1, count)
@@ -71,30 +73,33 @@
             barrier, inc=1, device_id={"dp": (me + distance) % count}, device_id_type=MESH
         )
 
-    reach_all(barrier, [{"seq": partner}] + [{"seq": (seat + 2 * k) % seats} for k in (1, 2, 3)])
+    reach_all(barrier, [{"seq": place} for place in (partner, right, left, across)])
     pl.semaphore_wait(barrier, count - 1 + 4)
 
-    def row_copy(distance):
-        peer = (me + distance) % count
+    def row_copy(turn):
+        peer = (me + far_first(turn, count)) % count
         return pltpu.make_async_remote_copy(
             src_ref=sent.at[peer],
-            dst_ref=got.at[me],
-            send_sem=out_sem.at[distance],
-            recv_sem=in_sem.at[distance],
+            dst_ref=got.at[turn],
+            send_sem=out_sem.at[turn],
+            recv_sem=in_sem.at[turn],
             device_id={"dp": peer},
             device_id_type=MESH,
         )
 
-    dp_exchange(count, lambda distance: row_copy(distance).start())
-    own = pltpu.make_async_copy(sent.at[me], got.at[me], own_sem.at[0])
+    @pl.loop(0, count - 1)
+    def _(turn):
+        row_copy(turn).start()
+
+    own = pltpu.make_async_copy(sent.at[me], got.at[count - 1], own_sem.at[0])
     own.start()
-    own_w = pltpu.make_async_copy(shard, full.at[seat], own_sem.at[1])
+    own_w = pltpu.make_async_copy(shard, full_w.at[seat], own_sem.at[1])
     own_w.start()
 
     def to_chip(k):
         return pltpu.make_async_remote_copy(
             src_ref=shard,
-            dst_ref=full.at[seat],
+            dst_ref=full_w.at[seat],
             send_sem=w_out.at[k],
             recv_sem=w_in.at[k],
             device_id={"seq": (seat + 2 * k) % seats},
@@ -102,7 +107,7 @@
         )
 
     def to_partner(k):
-        block = full.at[(seat + seats - 2 * k) % seats]
+        block = full_w.at[(seat + seats - 2 * k) % seats]
         return pltpu.make_async_remote_copy(
             src_ref=shard if k == 0 else block,
             dst_ref=block,
@@ -112,108 +117,116 @@
             device_id_type=MESH,
         )
 
+    def send(quarter, owner, target, out_sems, in_sems, slot):
+        block = full.at[quarter, owner]
+        return pltpu.make_async_remote_copy(
+            src_ref=block,
+            dst_ref=block,
+            send_sem=out_sems.at[quarter, slot],
+            recv_sem=in_sems.at[quarter, slot],
+            device_id={"seq": target},
+            device_id_type=MESH,
+        )
+
+    def ring(quarter, slot):
+        owner, target = [
+            (seat, right),
+            (seat, left),
+            (left, right) if 2 * quarter < quarters else (right, left),
+        ][slot]
+        return send(quarter, owner, target, ring_out, ring_in, slot)
+
+    def pair(quarter, slot):
+        return send(quarter, (seat, left, right, across)[slot], partner, pair_out, pair_in, slot)
+
+    def arrive(quarter):
+        @pl.loop(quarter * turns, min((quarter + 1) * turns, count - 1))
+        def _(turn):
+            row_copy(turn).wait_recv()
+
+        if quarter == quarters - 1:
+            own.wait()
+        arrived = got[quarter * turns : (quarter + 1) * turns].astype(jnp.float32)
+        arrived = arrived.reshape(rows, full.shape[3])
+        full[quarter, seat, :, :depth] = norm_rows(arrived[:, :depth], gain[...]).astype(jnp.bfloat16)
+        full[quarter, seat, :, depth:] = arrived[:, depth:].astype(jnp.bfloat16)
+        ring(quarter, 0).start()
+        ring(quarter, 1).start()
+        pair(quarter, 0).start()
+
+    def forward(quarter):
+        ring(quarter, 0).wait_recv()
+        if 2 * quarter < quarters:
+            ring(quarter, 2).start()
+        pair(quarter, 1).start()
+        ring(quarter, 1).wait_recv()
+        if 2 * quarter >= quarters:
+            ring(quarter, 2).start()
+        pair(quarter, 2).start()
+
+    def finish(quarter):
+        ring(quarter, 2).wait_recv()
+        pair(quarter, 3).start()
+        for slot in range(4):
+            pair(quarter, slot).wait_recv()
+        block = full[quarter, :, :, :depth].reshape(seats * rows, depth)
+        part = half_silu(0.5 * jnp.dot(block, w_ref[...], preferred_element_type=jnp.float32))
+        mixed[:, quarter] = part.astype(jnp.bfloat16).reshape(seats, rows, part.shape[1])
+
     for k in (1, 2, 3):
         to_chip(k).start()
     to_partner(0).start()
-    for k in (1, 3, 2):
-        to_chip(k).wait_recv()
-        to_partner(k).start()
+    for quarter in range(quarters):
+        arrive(quarter)
+        if quarter == 0:
+            for k in (1, 3, 2):
+                to_chip(k).wait_recv()
+                to_partner(k).start()
+        if quarter >= 1:
+            forward(quarter - 1)
+        if quarter >= 2:
+            finish(quarter - 2)
+    forward(quarters - 1)
+    finish(quarters - 2)
+    finish(quarters - 1)
+
+    total = quarters * rows
+    first = (lax.broadcasted_iota(jnp.int32, (8, 128), 1) == 0).astype(jnp.bfloat16)
+    places = lax.broadcasted_iota(jnp.int32, (total, total), 0).astype(jnp.float32)
+
+    @pl.loop(0, seats)
+    def _(owner):
+        tags = jnp.concatenate([full[quarter, owner, :, depth:] for quarter in range(quarters)], axis=0)
+        tag_row = lax.dot_general(
+            first, tags, (((1,), (1,)), ((), ())), preferred_element_type=jnp.float32
+        )[0:1]
+        chosen = (places == tag_row).astype(jnp.bfloat16)
+        arrived = mixed[owner].reshape(total, mixed.shape[3])
+        there = pl.ds(pl.multiple_of(owner * total, total), total)
+        proj[there, :] = jnp.dot(chosen, arrived, preferred_element_type=jnp.float32).astype(
+            jnp.bfloat16
+        )
+
+    tags = jnp.concatenate([full[quarter, seat, :, depth:] for quarter in range(quarters)], axis=0)
+    tags = jnp.concatenate([tags.astype(jnp.float32)] * (total // 128), axis=1)
+    columns = lax.broadcasted_iota(jnp.int32, (total, total), 1).astype(jnp.float32)
+    to_place[...] = (tags == columns).astype(jnp.bfloat16)
+
     for k in (1, 2, 3):
         to_chip(k).wait_send()
     for k in range(4):
         to_partner(k).wait()
-
-    @pl.loop(1, count)
-    def _(distance):
-        row_copy(distance).wait()
-
-    own.wait()
+    for quarter in range(quarters):
+        for slot in range(3):
+            ring(quarter, slot).wait_send()
+        for slot in range(4):
+            pair(quarter, slot).wait_send()
+
+    @pl.loop(0, count - 1)
+    def _(turn):
+        row_copy(turn).wait_send()
+
     own_w.wait()
-
-
-def gather_kernel(block_in, w_ref, proj, full, ring_out, ring_in, pair_out, pair_in):
-    seat = lax.axis_index("seq")
-    seats = lax.axis_size("seq")
-    partner = seat + 1 - 2 * (seat % 2)
-    right, left = (seat + 2) % seats, (seat + seats - 2) % seats
-    across = (seat + 4) % seats
-    rows = block_in.shape[0]
-    half = rows // 2
-    barrier = pltpu.get_barrier_semaphore()
-    reach_all(barrier, [{"seq": partner}, {"seq": right}, {"seq": left}])
-    pl.semaphore_wait(barrier, 3)
-
-    def piece(ref, part):
-        return ref.at[pl.ds(part * half, half)]
-
-    def ring(slot, source, owner, part, target):
-        return pltpu.make_async_remote_copy(
-            src_ref=piece(source, part),
-            dst_ref=piece(full.at[owner], part),
-            send_sem=ring_out.at[slot],
-            recv_sem=ring_in.at[slot],
-            device_id={"seq": target},
-            device_id_type=MESH,
-        )
-
-    def pair(slot, source, owner, part):
-        return pltpu.make_async_remote_copy(
-            src_ref=piece(source, part),
-            dst_ref=piece(full.at[owner], part),
-            send_sem=pair_out.at[slot],
-            recv_sem=pair_in.at[slot],
-            device_id={"seq": partner},
-            device_id_type=MESH,
-        )
-
-    firsts = [
-        ring(0, block_in, seat, 0, right),
-        ring(1, block_in, seat, 1, left),
-        ring(2, block_in, seat, 1, right),
-        ring(3, block_in, seat, 0, left),
-    ]
-    for copy in firsts:
-        copy.start()
-    pairs = [pair(0, block_in, seat, 0), pair(1, block_in, seat, 1)]
-    pairs[0].start()
-    pairs[1].start()
-    seconds = [
-        ring(4, full.at[left], left, 0, right),
-        ring(5, full.at[right], right, 1, left),
-    ]
-
-    def project(block, owner):
-        there = pl.ds(pl.multiple_of(owner * rows, rows), rows)
-        proj[there, :] = half_silu(
-            0.5 * jnp.dot(block[...], w_ref[...], preferred_element_type=jnp.float32)
-        ).astype(jnp.bfloat16)
-
-    project(block_in, seat)
-    pairs[0].wait_recv()
-    pairs[1].wait_recv()
-    project(full.at[partner], partner)
-    arrivals = [(left, 0), (right, 1), (left, 1), (right, 0), (across, 0), (across, 1)]
-    for slot, (owner, part) in enumerate(arrivals):
-        (firsts[slot] if slot < 4 else seconds[slot - 4]).wait_recv()
-        if slot < 2:
-            seconds[slot].start()
-        pairs.append(pair(2 + slot, full.at[owner], owner, part))
-        pairs[-1].start()
-        if slot == 3:
-            project(full.at[left], left)
-            project(full.at[right], right)
-            for early in (2, 3, 4, 5):
-                pairs[early].wait_recv()
-            for owner in (left, right):
-                other = owner + 1 - 2 * (owner % 2)
-                project(full.at[other], other)
-    project(full.at[across], across)
-    pairs[6].wait_recv()
-    pairs[7].wait_recv()
-    other = across + 1 - 2 * (across % 2)
-    project(full.at[other], other)
-    for copy in firsts + seconds + pairs:
-        copy.wait_send()
 
 
 def tail_kernel(
@@ -298,24 +311,27 @@
     for distance in range(1, seats):
         swap(distance).wait_send()
 
-    def back(distance):
-        peer = (me + distance) % peers
-        return pltpu.make_async_remote_copy(
-            src_ref=returned.at[peer],
+    def back(turn):
+        peer = (me + peers - far_first(turn, peers)) % peers
+        return pltpu.make_async_remote_copy(
+            src_ref=returned.at[turn],
             dst_ref=home.at[me],
-            send_sem=back_out.at[distance],
-            recv_sem=back_in.at[distance],
+            send_sem=back_out.at[turn],
+            recv_sem=back_in.at[turn],
             device_id={"dp": peer},
             device_id_type=MESH,
         )
 
-    dp_exchange(peers, lambda distance: back(distance).start())
-    own = pltpu.make_async_copy(returned.at[me], home.at[me], own_sem)
+    @pl.loop(0, peers - 1)
+    def _(turn):
+        back(turn).start()
+
+    own = pltpu.make_async_copy(returned.at[peers - 1], home.at[me], own_sem)
     own.start()
 
-    @pl.loop(1, peers)
-    def _(distance):
-        back(distance).wait()
+    @pl.loop(0, peers - 1)
+    def _(turn):
+        back(turn).wait()
 
     own.wait()
 
@@ -337,27 +353,34 @@
     )(*operands)
 
 
-def enter(sent, shard):
+def enter(sent, shard, gain, w_project, quarters=4):
     count, seats = lax.axis_size("dp"), lax.axis_size("seq")
+    peers, each, wide = sent.shape
+    rows, width = peers * each // quarters, w_project.shape[1]
     return remote(
-        functools.partial(enter_kernel, count),
+        functools.partial(enter_kernel, count, quarters),
         0,
-        (sent, shard),
-        (sent.shape, (seats,) + shard.shape),
-        [DMA((count,)), DMA((count,)), DMA((2,)), DMA((8,)), DMA((8,))],
+        (sent, shard, gain[None], w_project),
+        (
+            (seats,) + shard.shape,
+            (seats * quarters * rows, width),
+            (quarters * rows, quarters * rows),
+        ),
+        [
+            pltpu.VMEM(sent.shape, jnp.bfloat16),
+            pltpu.VMEM((quarters, seats, rows, wide), jnp.bfloat16),
+            pltpu.VMEM((seats, quarters, rows, width), jnp.bfloat16),
+            DMA((count,)),
+            DMA((count,)),
+            DMA((8,)),
+            DMA((8,)),
+            DMA((quarters, 3)),
+            DMA((quarters, 3)),
+            DMA((quarters, 4)),
+            DMA((quarters, 4)),
+            DMA((2,)),
+        ],
     )
-
-
-def gather(block, w_project):
-    seats = lax.axis_size("seq")
-    rows, depth = block.shape
-    return remote(
-        gather_kernel,
-        1,
-        (block, w_project),
-        ((seats * rows, w_project.shape[1]),),
-        [pltpu.VMEM((seats, rows, depth), jnp.bfloat16), DMA((6,)), DMA((6,)), DMA((8,)), DMA((8,))],
-    )[0]
 
 
 def tail(proj, table, gain, segment, w_full, to_place):
@@ -415,13 +438,9 @@
         [events[0], jnp.broadcast_to(owner_row[0][:, None], (count, 128)).astype(jnp.bfloat16)], axis=1
     )
     sent = pick(to_slot, tagged, 1)
-    got, w_full = enter(sent.reshape(peers, each, depth + 128), w_output)
-    got = got.reshape(count, depth + 128)
-    place = got[:, depth].astype(jnp.int32)
-    to_place = (place[:, None] == index[None, :]).astype(jnp.bfloat16)
-    normed = norm_rows(got[:, :depth].astype(jnp.float32), in_gain).astype(jnp.bfloat16)
-    normed = pick(to_place, normed, 0)
-    proj = gather(normed, w_project)
+    w_full, proj, to_place = enter(
+        sent.reshape(peers, each, depth + 128), w_output, in_gain, w_project
+    )
     home = tail(proj, rel_bias, out_gain, user_ids, w_full.reshape(-1, depth), to_place)
     home = home.reshape(count, depth)
     return pick(to_slot, home, 0)[None]

time: 131 us -> 128 us (0.977)
  local copies, waits for them, and re-layouts: 3.18 us -> 0.72 us
    unnamed x17 -> x12, local copies, waits for them, and re-layouts: 2.37 us -> 0.04 us
    pallas_call x2 -> x1, Pallas kernels: 71.9 us -> 72.5 us  [remote(): pl.pallas_call(kernel, out_shape=tuple((jax.ShapeDtypeStruct(shape, jnp.b...]
    dot_general x3 -> x2, matrix products: 3.05 us -> 2.63 us  [pick(): lax.dot_general(chosen, rows, (((dim,), (0,)), ((), ())), preferred_eleme...]
where the time goes in v4:
time: 128 us; the launch traced here: 127 us
  Pallas kernels  122 us (95%)
  matrix products  2.63 us (2%)
  other arithmetic  2.32 us (2%)
    pallas_call x1, Pallas kernels, remote(): pl.pallas_call(kernel, out_shape=tuple((jax.ShapeDtypeStruct(shape, jnp.b...  72.5 us
    pallas_call x1, Pallas kernels, tail(): pl.pallas_call(functools.partial(tail_kernel, count // 2, peers), out_sha...  49 us
    dot_general x2, matrix products, pick(): lax.dot_general(chosen, rows, (((dim,), (0,)), ((), ())), preferred_eleme...  2.63 us

profile of v4, /device:TPU:1, one launch (start us, length us, event | category | flops | bytes accessed | tf_op | source)
XLA Modules:
  0.0 127.3 jit_solution(2242255354933338780)
XLA Ops:
  0.0 0.9 convert_reduce_fusion
  0.9 0.7 multiply_add_fusion
  1.6 0.7 convert_reduce_fusion.1
  2.3 0.1 broadcast_in_dim.12
  2.4 0.0 copy-start
  2.4 0.0 copy-start.1
  2.4 0.0 copy-start.3
  2.5 1.5 %convolution_convert_fusion = bf16[256,1152]{1,0:T(8,128)(2,1)S(1)} fusion(bf16[256,128]{1,0:T(8,128)(2,1)S(1)} %broadcast_in_dim.12, bf16[256,1024]{1,0:T(8,128)(2,1)} %bitcast.19, s32[256]{0:T(256)S(1)} %bitcast.16), kind=kOutput, calls=%fused_computation | convolution fusion | flops 152535040 | bytes 1180672 | tf_op jit(solution)/shard_map/dot_general | solution.py:423
  3.9 0.1 reshape.15.sent
  4.1 0.0 copy-start.2
  4.1 0.0 copy-done
  4.1 0.0 copy-done.1
  4.1 0.0 copy-done.3
  4.1 0.0 copy-start.4
  4.1 0.0 copy-start.5
  4.2 72.5 %shard_map.91 = (bf16[8,128,1024]{2,1,0:T(8,128)(2,1)S(1)}, bf16[2048,512]{1,0:T(8,128)(2,1)S(1)}, bf16[256,256]{1,0:T(8,128)(2,1)S(1)}) custom-call(bf16[64,4,1152]{2,1,0:T(4,128)(2,1)S(1)} %reshape.15.sent, bf16[128,1024]{1,0:T(8,128)(2,1)S(1)} %copy-done.1, f32[1,1024]{1,0:T(1,128)S(1)} %bitcast.13, bf16[1024,512]{1,0:T(8,128)(2,1)S(1)} %copy-done), custom_call_target="tpu_custom_call" | custom-call | tf_op jit(solution)/shard_map/pallas_call | solution.py:344
  76.7 0.0 copy-done.2
  76.7 0.3 broadcast_in_dim.29.col_ids
  77.0 0.0 copy-done.4
  77.0 0.0 copy-done.5
  77.0 49.0 %shard_map.92 = bf16[64,4,1024]{2,1,0:T(4,128)(2,1)S(1)} custom-call(f32[1,11]{1,0:T(1,128)S(1)} %copy-done.4, bf16[2048,512]{1,0:T(8,128)(2,1)S(1)} %get-tuple-element.8.proj, f32[1,128]{1,0:T(1,128)S(1)} %bitcast.14, s32[1,2048]{1,0:T(1,128)S(1)} %copy-done.2, s32[2048,128]{1,0:T(8,128)S(1)} %broadcast_in_dim.29.col_ids, bf16[1024,1024]{1,0:T(8,128)(2,1)S(1)} %bitcast.11, ...), custom_call_target="tpu_custom_call" | custom-call | tf_op jit(solution)/shard_map/pallas_call | solution.py:391
  126.0 0.1 reshape.17
  126.2 1.1 fusion
Async XLA Ops:
  2.4 1.7 %copy-start = (bf16[1024,512]{1,0:T(8,128)(2,1)S(1)}, bf16[1024,512]{1,0:T(8,128)(2,1)}, u32[]{:S(2)}) copy-start(bf16[1024,512]{1,0:T(8,128)(2,1)} %w_ref.1) | copy-start | bytes 3145732
  2.4 1.7 %copy-start.1 = (bf16[128,1024]{1,0:T(8,128)(2,1)S(1)}, bf16[128,1024]{1,0:T(8,128)(2,1)}, u32[]{:S(2)}) copy-start(bf16[128,1024]{1,0:T(8,128)(2,1)} %shard.1) | copy-start | bytes 786436
  2.4 1.7 %copy-start.3 = (f32[1024]{0:T(1024)S(1)}, f32[1024]{0:T(1024)}, u32[]{:S(2)}) copy-start(f32[1024]{0:T(1024)} %param.13) | copy-start | bytes 12292
  4.1 72.6 %copy-start.2 = (s32[1,2048]{1,0:T(1,128)S(1)}, s32[1,2048]{1,0:T(1,128)}, u32[]{:S(2)}) copy-start(s32[1,2048]{1,0:T(1,128)} %row_ids.1) | copy-start | bytes 24580
  4.1 72.9 %copy-start.4 = (f32[1,11]{1,0:T(1,128)S(1)}, f32[1,11]{1,0:T(1,128)}, u32[]{:S(2)}) copy-start(f32[1,11]{1,0:T(1,128)} %table.1) | copy-start | bytes 136
  4.1 72.9 %copy-start.5 = (f32[128]{0:T(128)S(1)}, f32[128]{0:T(128)}, u32[]{:S(2)}) copy-start(f32[128]{0:T(128)} %param.14) | copy-start | bytes 1540

commit v5 on v4

--- a/solution.py
+++ b/solution.py
@@ -49,8 +49,9 @@
         pl.semaphore_signal(barrier, inc=1, device_id=place, device_id_type=MESH)
 
 
-def far_first(turn, count):
-    return count // 2 - (turn + 1) // 2 * (2 * (turn % 2) - 1)
+def near_first(turn, count):
+    mirrored = count - 2 - turn
+    return count // 2 - (mirrored + 1) // 2 * (2 * (mirrored % 2) - 1)
 
 
 def enter_kernel(
@@ -77,7 +78,7 @@
     pl.semaphore_wait(barrier, count - 1 + 4)
 
     def row_copy(turn):
-        peer = (me + far_first(turn, count)) % count
+        peer = (me + near_first(turn, count)) % count
         return pltpu.make_async_remote_copy(
             src_ref=sent.at[peer],
             dst_ref=got.at[turn],
@@ -312,7 +313,7 @@
         swap(distance).wait_send()
 
     def back(turn):
-        peer = (me + peers - far_first(turn, peers)) % peers
+        peer = (me + peers - near_first(turn, peers)) % peers
         return pltpu.make_async_remote_copy(
             src_ref=returned.at[turn],
             dst_ref=home.at[me],
@@ -324,7 +325,7 @@
 
     @pl.loop(0, peers - 1)
     def _(turn):
-        back(turn).start()
+        back(peers - 2 - turn).start()
 
     own = pltpu.make_async_copy(returned.at[peers - 1], home.at[me], own_sem)
     own.start()

time: 128 us -> 123 us (0.961)
  Pallas kernels: 122 us -> 117 us
    pallas_call x1, Pallas kernels: 72.5 us -> 65.4 us  [remote(): pl.pallas_call(kernel, out_shape=tuple((jax.ShapeDtypeStruct(shape, jnp.b...]
    pallas_call x1, Pallas kernels: 49 us -> 51.3 us  [tail(): pl.pallas_call(functools.partial(tail_kernel, count // 2, peers), out_sha...]
where the time goes in v5:
time: 123 us
  Pallas kernels  117 us (95%)
  matrix products  2.63 us (2%)
  other arithmetic  2.32 us (2%)
    pallas_call x1, Pallas kernels, remote(): pl.pallas_call(kernel, out_shape=tuple((jax.ShapeDtypeStruct(shape, jnp.b...  65.4 us
    pallas_call x1, Pallas kernels, tail(): pl.pallas_call(functools.partial(tail_kernel, count // 2, peers), out_sha...  51.3 us
    dot_general x2, matrix products, pick(): lax.dot_general(chosen, rows, (((dim,), (0,)), ((), ())), preferred_eleme...  2.63 us

profile of v5, /device:TPU:1, one launch (start us, length us, event | category | flops | bytes accessed | tf_op | source)
XLA Modules:
  0.0 122.5 jit_solution(8045163275722093118)
XLA Ops:
  0.0 0.9 convert_reduce_fusion
  0.9 0.7 multiply_add_fusion
  1.6 0.7 convert_reduce_fusion.1
  2.3 0.1 broadcast_in_dim.12
  2.4 0.0 copy-start
  2.4 0.0 copy-start.1
  2.4 0.0 copy-start.3
  2.5 1.5 %convolution_convert_fusion = bf16[256,1152]{1,0:T(8,128)(2,1)S(1)} fusion(bf16[256,128]{1,0:T(8,128)(2,1)S(1)} %broadcast_in_dim.12, bf16[256,1024]{1,0:T(8,128)(2,1)} %bitcast.19, s32[256]{0:T(256)S(1)} %bitcast.16), kind=kOutput, calls=%fused_computation | convolution fusion | flops 152535040 | bytes 1180672 | tf_op jit(solution)/shard_map/dot_general | solution.py:424
  3.9 0.1 reshape.15.sent
  4.1 0.0 copy-start.2
  4.1 0.0 copy-done
  4.1 0.0 copy-done.1
  4.1 0.0 copy-done.3
  4.1 0.0 copy-start.4
  4.1 0.0 copy-start.5
  4.2 65.4 %shard_map.91 = (bf16[8,128,1024]{2,1,0:T(8,128)(2,1)S(1)}, bf16[2048,512]{1,0:T(8,128)(2,1)S(1)}, bf16[256,256]{1,0:T(8,128)(2,1)S(1)}) custom-call(bf16[64,4,1152]{2,1,0:T(4,128)(2,1)S(1)} %reshape.15.sent, bf16[128,1024]{1,0:T(8,128)(2,1)S(1)} %copy-done.1, f32[1,1024]{1,0:T(1,128)S(1)} %bitcast.13, bf16[1024,512]{1,0:T(8,128)(2,1)S(1)} %copy-done), custom_call_target="tpu_custom_call" | custom-call | tf_op jit(solution)/shard_map/pallas_call | solution.py:345
  69.6 0.0 copy-done.2
  69.6 0.3 broadcast_in_dim.29.col_ids
  69.9 0.0 copy-done.4
  69.9 0.0 copy-done.5
  70.0 51.3 %shard_map.92 = bf16[64,4,1024]{2,1,0:T(4,128)(2,1)S(1)} custom-call(f32[1,11]{1,0:T(1,128)S(1)} %copy-done.4, bf16[2048,512]{1,0:T(8,128)(2,1)S(1)} %get-tuple-element.8.proj, f32[1,128]{1,0:T(1,128)S(1)} %bitcast.14, s32[1,2048]{1,0:T(1,128)S(1)} %copy-done.2, s32[2048,128]{1,0:T(8,128)S(1)} %broadcast_in_dim.29.col_ids, bf16[1024,1024]{1,0:T(8,128)(2,1)S(1)} %bitcast.11, ...), custom_call_target="tpu_custom_call" | custom-call | tf_op jit(solution)/shard_map/pallas_call | solution.py:392
  121.3 0.1 reshape.17
  121.4 1.1 fusion
Async XLA Ops:
  2.4 1.7 %copy-start = (bf16[1024,512]{1,0:T(8,128)(2,1)S(1)}, bf16[1024,512]{1,0:T(8,128)(2,1)}, u32[]{:S(2)}) copy-start(bf16[1024,512]{1,0:T(8,128)(2,1)} %w_ref.1) | copy-start | bytes 3145732
  2.4 1.7 %copy-start.1 = (bf16[128,1024]{1,0:T(8,128)(2,1)S(1)}, bf16[128,1024]{1,0:T(8,128)(2,1)}, u32[]{:S(2)}) copy-start(bf16[128,1024]{1,0:T(8,128)(2,1)} %shard.1) | copy-start | bytes 786436
  2.4 1.7 %copy-start.3 = (f32[1024]{0:T(1024)S(1)}, f32[1024]{0:T(1024)}, u32[]{:S(2)}) copy-start(f32[1024]{0:T(1024)} %param.13) | copy-start | bytes 12292
  4.1 65.5 %copy-start.2 = (s32[1,2048]{1,0:T(1,128)S(1)}, s32[1,2048]{1,0:T(1,128)}, u32[]{:S(2)}) copy-start(s32[1,2048]{1,0:T(1,128)} %row_ids.1) | copy-start | bytes 24580
  4.1 65.8 %copy-start.4 = (f32[1,11]{1,0:T(1,128)S(1)}, f32[1,11]{1,0:T(1,128)}, u32[]{:S(2)}) copy-start(f32[1,11]{1,0:T(1,128)} %table.1) | copy-start | bytes 136
  4.1 65.8 %copy-start.5 = (f32[128]{0:T(128)S(1)}, f32[128]{0:T(128)}, u32[]{:S(2)}) copy-start(f32[128]{0:T(128)} %param.14) | copy-start | bytes 1540
